TPU v7x, 256 devices: a whole 4x4x8 slice. The times are simulated.
256 devices in a mesh: dp: 2 (over z_hi), tensor: 4 (over y), pool: 32 (over x, z_lo, core).
Axes of the slice: x: 4, y: 4, z: 8 (z_hi: 2, z_lo: 4; z = z_hi * 4 + z_lo), core: 2. Of those that a mesh axis runs over, the one named last changes fastest.
Arguments:
- tokens: bfloat16 [64, 1024, 4096], P(('dp', 'pool')), may hold values from -192 to 192, as said below
- w_hidden: bfloat16 [4096, 4096], P('pool', 'tensor'), may hold values from -0.09375 to 0.09375
- w_out: bfloat16 [4096, 256], P('tensor'), may hold values from -0.09375 to 0.09375
- bank: bfloat16 [32768, 256], P('pool'), may hold values from -0.5 to 0.5
- item_ids: int32 [32768], P('pool'), may hold values from 0 to 1048575
- log_freq: bfloat16 [1048576], replicated, may hold values from -14 to -6
- positives: int32 [64, 1024], P(('dp', 'pool'), 'tensor'), may hold values from 0 to 32767
- new_items: bfloat16 [8192, 256], P('pool'), may hold values from -0.5 to 0.5
- new_owner: int32 [8192, 1], P('pool'), may hold values from 0 to 31; in each aligned block of 256 rows (0 to 255, 256 to 511, ...) at most 16 rows name the same one
- queue_head: int32 [32], P('pool'), may hold values from 0 to 1023
Outputs:
- query_loss: float32 [64, 1024], P(('dp', 'pool'), 'tensor')
- new_bank: bfloat16 [32768, 256], P('pool')
Inputs may be any that keep to these rules, and one draw needn't show every extreme that they name: `tokens`: float values within the range. `new_owner`: among the 256 new rows of one pool index, no shard is named by more than 16 rows, a bound that some block reaches.
All inputs are finite; a program needn't handle non-finite values.
Results may differ from a plain program's by a relative error of at most 0.002.
Values may be sent and summed in bfloat16 or wider, within the bound.
A program may use at most 128 MiB of HBM per device.

v0:
```python
import jax
import jax.numpy as jnp
from jax import lax
from jax.sharding import Mesh
from jax.sharding import PartitionSpec as P

POOL = ("pool_0", "pool_1", "pool_2")
DP_POOL = ("dp", "pool_0", "pool_1", "pool_2")


inv_temp = 5.0


def split_up(x, dim, count):
    before, after = (x.shape[:dim], x.shape[dim + 1 :])
    return jnp.moveaxis(x.reshape(*before, count, -1, *after), dim, 0)


def sum_at_owner(x, axis, dim):
    count = lax.axis_size(axis)
    blocks = lax.all_to_all(split_up(x, dim, count), axis, 0, 0, tiled=True)
    return jnp.sum(blocks, axis=0)


def all_in_one(x, axis):
    leaves = jax.tree.leaves(x)
    turns = sorted(range(len(leaves)), key=lambda k: -leaves[k].size)
    width = (1, *leaves[turns[0]].shape)[-1]
    lines = [
        jnp.pad(leaves[k].reshape(-1), (0, -leaves[k].size % width)).reshape(-1, width)
        for k in turns
    ]
    both, at, found = (lax.all_gather(jnp.concatenate(lines), axis), 0, {})
    for k, line in zip(turns, lines):
        section = both[:, at : at + len(line)].reshape(len(both), -1)
        found[k] = section[:, : leaves[k].size].reshape(-1, *leaves[k].shape)
        at += len(line)
    numbers = iter(range(len(leaves)))
    return jax.tree.map(lambda _: found[next(numbers)], x)


def joined_all(x, axes, combine):
    for axis in axes:
        pieces = all_in_one(x, axis)
        x = jax.tree.map(lambda part: part[0], pieces)
        for k in range(1, lax.axis_size(axis)):
            x = combine(x, jax.tree.map(lambda part: part[k], pieces))
    return x


def copy_for_each(x, axis):
    copies = jnp.broadcast_to(x, (lax.axis_size(axis), *x.shape))
    return lax.all_to_all(copies, axis, split_axis=0, concat_axis=0, tiled=True)


def folded_in_pairs(pieces, combine):
    while len(jax.tree.leaves(pieces)[0]) > 1:
        pieces = jax.vmap(combine)(*(pieces[side::2] for side in (0, 1)))
    return pieces[0]


def entering(x, axis, combine, identity):
    count, position = (lax.axis_size(axis), lax.axis_index(axis))
    passed = jnp.arange(count) < position

    def kept(part, zero, own):
        part = jnp.where(
            passed.reshape(-1, *(1 for _ in own.shape)), part, jnp.asarray(zero, own.dtype)
        )
        return part

    pieces = copy_for_each(x, axis)
    return folded_in_pairs(kept(pieces, identity, x), combine)


def local_stats(query_rows, target_rows, bank, offsets, base_column):
    row_count = query_rows.shape[0]
    bank_rows = bank.shape[0]
    block_width = 512
    block_count = bank_rows // block_width
    blocks = bank.reshape(block_count, block_width, bank.shape[1])
    shifts = offsets.reshape(block_count, block_width)

    def block_step(running, inputs):
        run_max, run_sum, run_pos = running
        bank_block, block_offsets, block_index = inputs
        logits = (
            inv_temp * jnp.dot(query_rows, bank_block.T, preferred_element_type=jnp.float32)
            - block_offsets[None, :]
        )
        next_max = jnp.maximum(run_max, jnp.max(logits, axis=1))
        run_sum = run_sum * jnp.exp(run_max - next_max) + jnp.sum(
            jnp.exp(logits - next_max[:, None]), axis=1
        )
        columns = base_column + block_index * block_width + jnp.arange(block_width, dtype=jnp.int32)
        run_pos = run_pos + jnp.sum(
            jnp.where(columns[None, :] == target_rows[:, None], logits, 0.0), axis=1
        )
        return ((next_max, run_sum, run_pos), None)

    initial = (
        jnp.full((row_count,), -jnp.inf, jnp.float32),
        jnp.zeros((row_count,), jnp.float32),
        jnp.zeros((row_count,), jnp.float32),
    )
    final, _ = lax.scan(
        block_step, initial, (blocks, shifts, jnp.arange(block_count, dtype=jnp.int32))
    )
    return final


def combine(earlier_part, later_part):
    both_max = jnp.maximum(earlier_part[0], later_part[0])
    both_sum = earlier_part[1] * jnp.exp(earlier_part[0] - both_max) + later_part[1] * jnp.exp(
        later_part[0] - both_max
    )
    return (both_max, both_sum, earlier_part[2] + later_part[2])


def add_counts(earlier_part, later_part):
    return earlier_part + later_part


def body(
    tokens, w_hidden, w_out, bank, item_ids, log_freq, positives, new_items, new_owner, queue_head
):
    token_rows = tokens[0]
    pre_act = jnp.dot(
        token_rows,
        lax.all_gather(w_hidden, POOL, axis=0, tiled=True),
        preferred_element_type=jnp.float32,
    )
    hidden = jnp.maximum(pre_act, 0.0).astype(jnp.bfloat16)
    partial_value = jnp.dot(hidden, w_out, preferred_element_type=jnp.float32)
    queries = sum_at_owner(partial_value, "tensor", 0).astype(jnp.bfloat16)
    offsets = jnp.take(log_freq, item_ids).astype(jnp.float32)
    own_index = lax.axis_index(POOL)
    base_column = own_index * bank.shape[0]
    query_piece = lax.all_gather(queries[None], POOL, axis=0, tiled=True)
    target_piece = lax.all_gather(positives, POOL, axis=0, tiled=True)
    groups_in = query_piece.shape[0]
    run_max, run_sum, run_pos = local_stats(
        query_piece.reshape(-1, query_piece.shape[2]),
        target_piece.reshape(-1),
        bank,
        offsets,
        base_column,
    )
    maxima = run_max.reshape(groups_in, -1)
    totals = run_sum.reshape(groups_in, -1)
    scores = run_pos.reshape(groups_in, -1)
    maxima, totals, scores = (maxima, totals, scores)
    maxima, totals, scores = joined_all((maxima, totals, scores), POOL, combine)
    own_max = lax.dynamic_slice_in_dim(maxima, own_index, 1, 0)
    own_sum = lax.dynamic_slice_in_dim(totals, own_index, 1, 0)
    own_pos = lax.dynamic_slice_in_dim(scores, own_index, 1, 0)
    query_loss = own_max + jnp.log(own_sum) - own_pos
    owners = new_owner[:, 0]
    head_slot = queue_head[0]
    shard_rows = bank.shape[0]
    peer_count = lax.axis_size(POOL)
    local_rows = new_items.shape[0]
    capacity = 2 * local_rows // peer_count
    onehot = (owners[:, None] == jnp.arange(peer_count, dtype=jnp.int32)[None, :]).astype(jnp.int32)
    counts = jnp.sum(onehot, axis=0, dtype=jnp.int32)
    before = jnp.sum(
        (jnp.cumsum(onehot, axis=0, dtype=jnp.int32) - onehot) * onehot, axis=1, dtype=jnp.int32
    )
    earlier = entering(counts, POOL, add_counts, jnp.zeros_like(counts))
    ranks = before + jnp.sum(onehot * earlier[None, :], axis=1, dtype=jnp.int32)
    send_pos = owners * capacity + before
    rows_out = (
        jnp.zeros((peer_count * capacity, new_items.shape[1]), jnp.bfloat16)
        .at[send_pos]
        .set(new_items)
    )
    ranks_out = jnp.full((peer_count * capacity,), -1, jnp.int32).at[send_pos].set(ranks)
    rows_in, ranks_in = (
        lax.all_to_all(
            rows_out.reshape(peer_count, capacity, -1),
            POOL,
            split_axis=0,
            concat_axis=0,
            tiled=True,
        ),
        lax.all_to_all(
            ranks_out.reshape(peer_count, capacity), POOL, split_axis=0, concat_axis=0, tiled=True
        ),
    )
    local_slots = jnp.where(ranks_in >= 0, (head_slot + ranks_in) % shard_rows, shard_rows).reshape(
        -1
    )
    new_bank = bank.at[local_slots].set(rows_in.reshape(-1, new_items.shape[1]), mode="drop")
    return (query_loss, new_bank)


def solution(mesh):
    finer = Mesh(
        mesh.devices.reshape(mesh.shape["dp"], mesh.shape["tensor"], 4, 4, 2),
        ("dp", "tensor", "pool_0", "pool_1", "pool_2"),
    )
    in_specs = (
        P(DP_POOL, None, None),
        P(POOL, "tensor"),
        P("tensor", None),
        P(POOL, None),
        P(POOL),
        P(),
        P(DP_POOL, "tensor"),
        P(POOL, None),
        P(POOL, None),
        P(POOL),
    )
    out_specs = (P(DP_POOL, "tensor"), P(POOL, None))
    return jax.shard_map(body, mesh=finer, in_specs=in_specs, out_specs=out_specs, check_vma=False)
```

profile of v0, /device:TPU:2, one launch (start us, length us, event | category | flops | bytes accessed | tf_op | source)
XLA Modules:
  0.0 273.2 jit_solution(2599973721477552642)
XLA Ops:
  7.2 0.7 all-gather.8.cloned.1.call-update
  8.0 73.3 %all-gather.8.cloned.1.call-done = bf16[4096,1024]{1,0:T(8,128)(2,1)} async-done(((bf16[128,1024]{1,0:T(8,128)(2,1)}), bf16[4096,1024]{1,0:T(8,128)(2,1)}) %all-gather.8.cloned.1.call-update) | async-done | bytes 8388624 | tf_op jit(solution)/shard_map/all_gather | solution.py:130
  81.3 16.4 %fusion.12 = f32[1024,256]{1,0:T(8,128)} fusion(bf16[1024,256]{1,0:T(8,128)(2,1)} %param.14, bf16[4096,1024]{1,0:T(8,128)(2,1)} %all-gather.8.cloned.1.call-done, bf16[1,1024,4096]{2,1,0:T(8,128)(2,1)} %param.12), kind=kOutput, calls=%fused_computation.22 | convolution fusion | flops 9128902656 | bytes 18350080 | tf_op jit(solution)/shard_map/dot_general | solution.py:134
  97.7 20.1 %all_to_all.28 = f32[4,256,256]{2,1,0:T(8,128)} all-to-all(f32[4,256,256]{2,1,0:T(8,128)} %bitcast.252), channel_id=1, replica_groups=mesh['dp'=2,'tensor'=4,'pool_0'=4,'pool_1'=4,'pool_2'=2] {'tensor'}, dimensions={0} | all-to-all | bytes 2097152 | tf_op jit(solution)/shard_map/all_to_all | solution.py:21
  117.7 2.0 reduce_sum.56
  119.7 0.1 convert_reduce_fusion
  119.9 0.6 broadcast_in_dim.52
  120.5 5.8 %all-to-all-start.1 = ((s32[32,1,32]{2,1,0:T(1,128)}), s32[32,1,32]{2,1,0:T(1,128)S(1)}, u32[]{:S(2)}, u32[]{:S(2)}) async-start(s32[32,1,32]{2,1,0:T(1,128)} %broadcast_in_dim.52), calls=%async_computation.1 | async-start | bytes 32768 | tf_op jit(solution)/shard_map/all_to_all | solution.py:53
  126.3 6.8 %gather_fusion = bf16[1024]{0:T(1024)(128)(2,1)S(1)} fusion(bf16[1048576]{0:T(1024)(128)(2,1)S(1)} %copy-done, s32[1024]{0:T(1024)S(1)} %fusion.46), kind=kCustom, calls=%fused_computation | custom fusion | bytes 8192 | tf_op jit(solution)/shard_map/jit(_take)/gather | solution.py:136
  133.2 0.6 reduce-window.6
  133.8 0.2 slice_reduce_fusion
  134.3 0.1 select_reduce_fusion
  134.4 1.4 scatter_custom_fusion
  135.8 0.7 all_to_all.21
  136.5 7.7 %all-to-all-start.2 = ((s32[32,1,16]{2,1,0:T(1,128)}), s32[32,1,16]{2,1,0:T(1,128)S(1)}, u32[]{:S(2)}, u32[]{:S(2)}) async-start(s32[32,1,16]{2,1,0:T(1,128)} %bitcast.37), calls=%async_computation.2 | async-start | bytes 32768 | tf_op jit(solution)/shard_map/all_to_all | solution.py:186
  144.2 36.4 %all-gather.4 = s32[32,1,256]{2,1,0:T(1,128)S(1)} all-gather(s32[1,1,256]{2,1,0:T(1,128)S(1)} %bitcast.259), channel_id=1, replica_groups=mesh['dp'=2,'tensor'=4,'pool_0'=4,'pool_1'=4,'pool_2'=2] {'pool_0','pool..., dimensions={0}, use_global_device_ids=true | all-gather | bytes 33792 | tf_op jit(solution)/shard_map/all_gather | solution.py:140
  181.3 2.5 scatter_custom_fusion.1
  183.8 11.1 %all-to-all-start.3 = ((bf16[32,16,256]{2,1,0:T(8,128)(2,1)}), bf16[32,16,256]{2,1,0:T(8,128)(2,1)S(1)}, u32[]{:S(2)}, u32[]{:S(2)}) async-start(bf16[32,16,256]{2,1,0:T(8,128)(2,1)} %bitcast.40), calls=%async_computation.3 | async-start | bytes 524288 | tf_op jit(solution)/shard_map/all_to_all | solution.py:179
  194.9 0.1 ge.29
  195.2 37.4 %while.15 = (s32[]{:T(128)}, f32[8192]{0:T(1024)S(1)}, f32[8192]{0:T(1024)S(1)}, f32[8192]{0:T(1024)S(1)}, bf16[2,512,256]{2,1,0:T(8,128)(2,1)S(1)}, /*index=5*/...) while((s32[]{:T(128)}, f32[8192]{0:T(1024)S(1)}, ...), condition=%wide.region_5.6_spmd.clone, body=%wide.region_1.5_spmd.clone.sunk | while | flops 2181087744 | bytes 38676668 | solution.py:106
  195.3 9.2 %fusion.74 = (f32[8192]{0:T(1024)S(1)}, f32[512,8192]{1,0:T(8,128)}) fusion(f32[512]{0:T(512)S(1)} %bitcast.241, bf16[8192,256]{1,0:T(8,128)(2,1)} %get-tuple-element.234, bf16[2,512,256]{2,1,0:T(8,128)(2,1)S(1)} %get-tuple-element.233, s32[]{:T(128)S(6)} %copy.27), kind=kOutput, calls=%fused_computation.130.clone.1 | convolution fusion | flops 2160058368 | bytes 21268484 | tf_op jit(solution)/shard_map/while/body/eval_jaxpr/dot_general | solution.py:88
  204.5 0.6 dynamic_slice.94
  205.8 8.1 %fusion.75 = (f32[8192]{0:T(1024)S(1)}, f32[8192]{0:T(1024)S(1)}) fusion(f32[512,8192]{1,0:T(8,128)} %get-tuple-element.198, s32[8192]{0:T(1024)S(1)} %bitcast.242, s32[512]{0:T(512)S(1)} %iota_add_fusion.2, f32[8192]{0:T(1024)S(1)} %select_maximum_fusion.2), kind=kLoop, calls=%fused_computation.8.clone.1 | loop fusion | flops 20955136 | bytes 16910336 | tf_op jit(solution)/shard_map/while/body/eval_jaxpr/reduce_sum | solution.py:96
  213.9 9.2 %fusion.74 = (f32[8192]{0:T(1024)S(1)}, f32[512,8192]{1,0:T(8,128)}) fusion(f32[512]{0:T(512)S(1)} %bitcast.241, bf16[8192,256]{1,0:T(8,128)(2,1)} %get-tuple-element.234, bf16[2,512,256]{2,1,0:T(8,128)(2,1)S(1)} %get-tuple-element.233, s32[]{:T(128)S(6)} %copy.27), kind=kOutput, calls=%fused_computation.130.clone.1 | convolution fusion | flops 2160058368 | bytes 21268484 | tf_op jit(solution)/shard_map/while/body/eval_jaxpr/dot_general | solution.py:88
  223.2 0.6 dynamic_slice.94
  224.4 8.1 %fusion.75 = (f32[8192]{0:T(1024)S(1)}, f32[8192]{0:T(1024)S(1)}) fusion(f32[512,8192]{1,0:T(8,128)} %get-tuple-element.198, s32[8192]{0:T(1024)S(1)} %bitcast.242, s32[512]{0:T(512)S(1)} %iota_add_fusion.2, f32[8192]{0:T(1024)S(1)} %select_maximum_fusion.2), kind=kLoop, calls=%fused_computation.8.clone.1 | loop fusion | flops 20955136 | bytes 16910336 | tf_op jit(solution)/shard_map/while/body/eval_jaxpr/reduce_sum | solution.py:96
  232.7 13.0 %all-gather.1 = f32[384,256]{1,0:T(8,128)S(1)} all-gather(f32[96,256]{1,0:T(8,128)S(1)} %pad_maximum_fusion), channel_id=3, replica_groups=mesh['dp'=2,'tensor'=4,'pool_0'=4,'pool_1'=4,'pool_2'=2] {'pool_0'}, dimensions={0}, use_global_device_ids=true | all-gather | bytes 491520 | tf_op jit(solution)/shard_map/all_gather | solution.py:33
  245.8 15.1 %all-gather.2 = f32[384,256]{1,0:T(8,128)S(1)} all-gather(f32[96,256]{1,0:T(8,128)S(1)} %pad_maximum_fusion.1), channel_id=4, replica_groups=mesh['dp'=2,'tensor'=4,'pool_0'=4,'pool_1'=4,'pool_2'=2] {'pool_1'}, dimensions={0}, use_global_device_ids=true | all-gather | bytes 491520 | tf_op jit(solution)/shard_map/all_gather | solution.py:33
  261.0 1.9 all-gather.3
  263.0 2.6 scatter_fusion
  265.6 0.7 fusion.54
  266.3 0.1 copy-done.1
  (74 shorter events, 1.0 us)
Async XLA Ops:
  7.2 119.2 %copy-start = (bf16[1048576]{0:T(1024)(128)(2,1)S(1)}, bf16[1048576]{0:T(1024)(128)(2,1)}, u32[]{:S(2)}) copy-start(bf16[1048576]{0:T(1024)(128)(2,1)} %param.17) | copy-start | bytes 6291460
  7.2 74.1 %all-gather.8.cloned.1.call-start = ((), (), s32[]{:S(2)}) async-start(), calls=%async_computation.4 | async-start | bytes 8650752 | tf_op jit(solution)/shard_map/all_gather | solution.py:130
  7.9 111.8 %copy-start.4 = (s32[256,1]{0,1:T(1,128)S(1)}, s32[256,1]{0,1:T(1,128)}, u32[]{:S(2)}) copy-start(s32[256,1]{0,1:T(1,128)} %param.20) | copy-start | bytes 3076
  7.9 118.4 %copy-start.3 = (s32[1024]{0:T(1024)S(1)}, s32[1024]{0:T(1024)}, u32[]{:S(2)}) copy-start(s32[1024]{0:T(1024)} %param.16) | copy-start | bytes 12292
  7.9 136.3 %copy-start.5 = (s32[1,256]{1,0:T(1,128)S(1)}, s32[1,256]{1,0:T(1,128)}, u32[]{:S(2)}) copy-start(s32[1,256]{1,0:T(1,128)} %param.18) | copy-start | bytes 3076
  7.9 187.3 %copy-start.2 = (bf16[1024,256]{1,0:T(8,128)(2,1)S(1)}, bf16[1024,256]{1,0:T(8,128)(2,1)}, u32[]{:S(2)}) copy-start(bf16[1024,256]{1,0:T(8,128)(2,1)} %param.15) | copy-start | bytes 1572868
  8.0 187.2 %all-gather.10.cloned.1.call-start = ((), (), s32[]{:S(2)}) async-start(), calls=%async_computation.5 | async-start | bytes 4325376 | tf_op jit(solution)/shard_map/all_gather | solution.py:139
  120.5 13.6 %all-to-all-start.1 = ((s32[32,1,32]{2,1,0:T(1,128)}), s32[32,1,32]{2,1,0:T(1,128)S(1)}, u32[]{:S(2)}, u32[]{:S(2)}) async-start(s32[32,1,32]{2,1,0:T(1,128)} %broadcast_in_dim.52), calls=%async_computation.1 | async-start | bytes 32768 | tf_op jit(solution)/shard_map/all_to_all | solution.py:53
  136.5 47.3 %all-to-all-start.2 = ((s32[32,1,16]{2,1,0:T(1,128)}), s32[32,1,16]{2,1,0:T(1,128)S(1)}, u32[]{:S(2)}, u32[]{:S(2)}) async-start(s32[32,1,16]{2,1,0:T(1,128)} %bitcast.37), calls=%async_computation.2 | async-start | bytes 32768 | tf_op jit(solution)/shard_map/all_to_all | solution.py:186
  183.8 79.2 %all-to-all-start.3 = ((bf16[32,16,256]{2,1,0:T(8,128)(2,1)}), bf16[32,16,256]{2,1,0:T(8,128)(2,1)S(1)}, u32[]{:S(2)}, u32[]{:S(2)}) async-start(bf16[32,16,256]{2,1,0:T(8,128)(2,1)} %bitcast.40), calls=%async_computation.3 | async-start | bytes 524288 | tf_op jit(solution)/shard_map/all_to_all | solution.py:179
  265.6 0.8 copy-start.1
Sparse Core Ops, SparseCore 0:
  9.8 71.4 all-gather.7
  119.9 59.5 all-gather.9
where the time goes:
time: 275 us; the launch traced here: 273 us
  blocking collectives  86.5 us (31%)
  waiting for transfers between devices  74 us (27%)
  matrix products  34.8 us (13%)
  starting transfers between devices  24.7 us (9%)
  other arithmetic  20.1 us (7%)
  local copies, waits for them, and re-layouts  16.6 us (6%)
  between operations  15 us (5%)
    all_gather x1, waiting for transfers between devices, body(): lax.all_gather(w_hidden, POOL, axis=0, tiled=True)  73.3 us
    all_gather x1, blocking collectives, body(): target_piece = lax.all_gather(positives, POOL, axis=0, tiled=True)  36.4 us
    all_gather x3, blocking collectives, all_in_one(): both, at, found = (lax.all_gather(jnp.concatenate(lines), axis), 0, {})  30.1 us
    all_to_all x1, blocking collectives, sum_at_owner(): blocks = lax.all_to_all(split_up(x, dim, count), axis, 0, 0, tiled=True)  20.1 us
    dot_general x2, matrix products, block_step(): jnp.dot(query_rows, bank_block.T, preferred_element_type=jnp.float32)  18.5 us
    dot_general x1, matrix products, body(): partial_value = jnp.dot(hidden, w_out, preferred_element_type=jnp.float32)  16.4 us
    reduce_sum x2, other arithmetic, block_step(): jnp.sum(jnp.where(columns[None, :] == target_rows[:, None], logits, 0.0),...  16.2 us
    all_to_all x1, starting transfers between devices, body(): lax.all_to_all(rows_out.reshape(peer_count, capacity, -1), POOL, split_ax...  11.1 us
  transfers between devices with their start and end apart: 5, of which 1 were waited for; matrix products, arithmetic and copies ran while one was open for 18% of the time, Pallas kernels for 0%

commit v1 on v0

--- a/solution.py
+++ b/solution.py
@@ -1,8 +1,15 @@
+import functools
 import jax
 import jax.numpy as jnp
 from jax import lax
+from jax.experimental import pallas as pl
+from jax.experimental.pallas import tpu as pltpu
+
+AXES = ("dp", "tensor", "pool_0", "pool_1", "pool_2")
 from jax.sharding import Mesh
 from jax.sharding import PartitionSpec as P
+
+MESH = pl.DeviceIdType.MESH
 
 POOL = ("pool_0", "pool_1", "pool_2")
 DP_POOL = ("dp", "pool_0", "pool_1", "pool_2")
@@ -121,17 +128,221 @@
     return earlier_part + later_part
 
 
+def tower_kernel(tok_hbm, w_hbm, wo_ref, out_ref, tok, wbuf, acc, tok_sem, own_sem, send_sem, recv_sem, psend, precv):
+    dp, y, x, zl, c = (lax.axis_index(a) for a in AXES)
+    pz = dp * 4 + zl
+    R = w_hbm.shape[0]
+    C = w_hbm.shape[1] // 2
+    Q = C // 2
+    M = tok.shape[1]
+    offs = (0, -1, 1, 2)
+
+    def chip(dx, dz):
+        xx = lax.rem(x + dx + 4, 4)
+        zz = lax.rem(pz + dz + 8, 8)
+        return (zz // 4, y, xx, lax.rem(zz, 4), c)
+
+    def along(h, first, step):
+        return chip(step, 0) if (h == 0) == first else chip(0, step)
+
+    partner = (dp, y, x, zl, 1 - c)
+
+    def block_of(h, f, s):
+        dx = f * (1 - h) + s * h
+        dz = s * (1 - h) + f * h
+        return lax.rem(x + dx + 4, 4) * 4 + lax.rem(zl + dz + 4, 4)
+
+    def view(h, f, s, piece, core):
+        row = pl.multiple_of(block_of(h, f, s) * (2 * R) + core * R, R)
+        cols = slice(None) if piece is None else pl.ds(piece * Q, Q)
+        return wbuf.at[h, pl.ds(row, R), cols]
+
+    def key(h, f, s, piece):
+        return ((h * 4 + offs.index(f)) * 4 + offs.index(s)) * 2 + (piece or 0)
+
+    sends = []
+
+    def send(h, f, s, piece, first, step, kind):
+        nf, ns = kind
+        ref = view(h, f, s, piece, c)
+        cp = pltpu.make_async_remote_copy(
+            src_ref=ref, dst_ref=ref, send_sem=send_sem.at[len(sends)],
+            recv_sem=recv_sem.at[key(h, nf, ns, piece)],
+            device_id=along(h, first, step), device_id_type=MESH)
+        cp.start()
+        sends.append(cp)
+
+    psends = []
+
+    def to_partner(h, f, s, piece):
+        ref = view(h, f, s, piece, c)
+        cp = pltpu.make_async_remote_copy(
+            src_ref=ref, dst_ref=ref, send_sem=psend.at[key(h, f, s, piece)],
+            recv_sem=precv.at[key(h, f, s, piece)], device_id=partner, device_id_type=MESH)
+        cp.start()
+        psends.append(cp)
+
+    def wait_link(h, f, s, piece):
+        ref = view(h, f, s, piece, c)
+        pltpu.make_async_remote_copy(
+            src_ref=ref, dst_ref=ref, send_sem=send_sem.at[0],
+            recv_sem=recv_sem.at[key(h, f, s, piece)], device_id=partner, device_id_type=MESH).wait_recv()
+
+    def wait_partner(h, f, s, piece):
+        ref = view(h, f, s, piece, 1 - c)
+        pltpu.make_async_remote_copy(
+            src_ref=ref, dst_ref=ref, send_sem=send_sem.at[0],
+            recv_sem=precv.at[key(h, f, s, piece)], device_id=partner, device_id_type=MESH).wait_recv()
+
+    def pieces(f, s):
+        return (0, 1) if (f == 2 and s == 0) or s == 2 else (None,)
+
+    own = [pltpu.make_async_copy(w_hbm.at[:, pl.ds(h * C, C)], view(h, 0, 0, None, c), own_sem.at[h]) for h in (0, 1)]
+    for cp in own:
+        cp.start()
+
+    barrier = pltpu.get_barrier_semaphore()
+    peers = [chip(1, 0), chip(-1, 0), chip(0, 1), chip(0, -1), partner]
+    for p in peers:
+        pl.semaphore_signal(barrier, inc=1, device_id=p, device_id_type=MESH)
+
+    groups = [[(0, 0)], [(-1, 0), (1, 0)], [(0, -1), (0, 1)], [(2, 0)],
+              [(-1, -1), (-1, 1), (1, -1), (1, 1)], [(0, 2)], [(2, -1), (2, 1)], [(-1, 2), (1, 2)], [(2, 2)]]
+
+    tok_wait = {}
+    n = 0
+    for g in groups:
+        for f, s in g:
+            for h in (0, 1):
+                dx, dz = (f, s) if h == 0 else (s, f)
+                if (dx, dz) in tok_wait:
+                    continue
+                b = block_of(0, dx, dz)
+                cp = pltpu.make_async_copy(
+                    tok_hbm.at[0, :, pl.ds(pl.multiple_of(b * 2 * R, 2 * R), 2 * R)], tok.at[b], tok_sem.at[n])
+                cp.start()
+                tok_wait[(dx, dz)] = cp
+                n += 1
+
+    for cp in own:
+        cp.wait()
+    pl.semaphore_wait(barrier, len(peers))
+
+    for h in (0, 1):
+        for step in (1, -1):
+            send(h, 0, 0, None, True, step, (-step, 0))
+    for h in (0, 1):
+        to_partner(h, 0, 0, None)
+    for h in (0, 1):
+        for step in (1, -1):
+            send(h, 0, 0, None, False, step, (0, -step))
+
+    def relay(g):
+        for f, s in groups[g]:
+            for h in (0, 1):
+                for p in pieces(f, s):
+                    wait_link(h, f, s, p)
+                if s == 0 and f != 2:
+                    send(h, f, 0, 0 if f == -1 else 1, True, -f, (2, 0))
+                if s == 0:
+                    for step in (1, -1):
+                        send(h, f, 0, None, False, step, (f, -step))
+                elif s != 2:
+                    send(h, f, s, 0 if s == -1 else 1, False, -s, (f, 2))
+                for p in pieces(f, s):
+                    to_partner(h, f, s, p)
+
+    def mm(g):
+        items = groups[g]
+        for f, s in items:
+            for h in (0, 1):
+                dx, dz = (f, s) if h == 0 else (s, f)
+                if (dx, dz) in tok_wait:
+                    tok_wait.pop((dx, dz)).wait()
+                for p in pieces(f, s):
+                    wait_partner(h, f, s, p)
+
+        def step(i, carry):
+            h = lax.rem(i, 2)
+            j = i // 2
+            f = sum(jnp.where(j == k, fs[0], 0) for k, fs in enumerate(items))
+            s = sum(jnp.where(j == k, fs[1], 0) for k, fs in enumerate(items))
+            b = block_of(h, f, s)
+            row = pl.multiple_of(b * (2 * R), 2 * R)
+            d = jnp.dot(tok[b], wbuf[h, pl.ds(row, 2 * R), :], preferred_element_type=jnp.float32)
+            if g == 0:
+                acc[h] = d
+            else:
+                acc[h] = acc[h] + d
+            return carry
+
+        lax.fori_loop(0, 2 * len(items), step, 0)
+
+    relay(1)
+    mm(0)
+    relay(2)
+    mm(1)
+    relay(3)
+    mm(2)
+    mm(3)
+    relay(4)
+    mm(4)
+    relay(5)
+    mm(5)
+    relay(6)
+    mm(6)
+    relay(7)
+    mm(7)
+    relay(8)
+    mm(8)
+
+    T = min(256, M)
+
+    def out_step(r, carry):
+        rs = pl.ds(pl.multiple_of(r * T, T), T)
+        total = None
+        for h in (0, 1):
+            hid = jnp.maximum(acc[h, rs, :], 0.0).astype(jnp.bfloat16)
+            d = jnp.dot(hid, wo_ref[pl.ds(h * C, C), :], preferred_element_type=jnp.float32)
+            total = d if total is None else total + d
+        out_ref[rs, :] = total
+        return carry
+
+    lax.fori_loop(0, M // T, out_step, 0)
+
+    for cp in sends + psends:
+        cp.wait_send()
+
+
+def tower(tokens, w_hidden, w_out):
+    M, K = tokens.shape[1:]
+    R, N = w_hidden.shape
+    E = w_out.shape[1]
+    return pl.pallas_call(
+        tower_kernel,
+        out_shape=jax.ShapeDtypeStruct((M, E), jnp.float32),
+        in_specs=[pl.BlockSpec(memory_space=pl.ANY), pl.BlockSpec(memory_space=pl.ANY), pl.BlockSpec(memory_space=pltpu.VMEM)],
+        out_specs=pl.BlockSpec(memory_space=pltpu.VMEM),
+        scratch_shapes=[
+            pltpu.VMEM((16, M, 2 * R), jnp.bfloat16),
+            pltpu.VMEM((2, K, N // 2), jnp.bfloat16),
+            pltpu.VMEM((2, M, N // 2), jnp.float32),
+            pltpu.SemaphoreType.DMA((16,)),
+            pltpu.SemaphoreType.DMA((2,)),
+            pltpu.SemaphoreType.DMA((46,)),
+            pltpu.SemaphoreType.DMA((64,)),
+            pltpu.SemaphoreType.DMA((64,)),
+            pltpu.SemaphoreType.DMA((64,)),
+        ],
+        compiler_params=pltpu.CompilerParams(collective_id=0, has_side_effects=True, vmem_limit_bytes=50 * 1024 * 1024),
+        name="tower",
+    )(tokens, w_hidden, w_out)
+
+
 def body(
     tokens, w_hidden, w_out, bank, item_ids, log_freq, positives, new_items, new_owner, queue_head
 ):
-    token_rows = tokens[0]
-    pre_act = jnp.dot(
-        token_rows,
-        lax.all_gather(w_hidden, POOL, axis=0, tiled=True),
-        preferred_element_type=jnp.float32,
-    )
-    hidden = jnp.maximum(pre_act, 0.0).astype(jnp.bfloat16)
-    partial_value = jnp.dot(hidden, w_out, preferred_element_type=jnp.float32)
+    partial_value = tower(tokens, w_hidden, w_out)
     queries = sum_at_owner(partial_value, "tensor", 0).astype(jnp.bfloat16)
     offsets = jnp.take(log_freq, item_ids).astype(jnp.float32)
     own_index = lax.axis_index(POOL)

time: 275 us -> 233 us (0.85)
  waiting for transfers between devices: 74 us -> 0.04 us
  Pallas kernels: 0 us -> 42.1 us
  matrix products: 34.8 us -> 18.5 us
    all_gather x1 -> x0, waiting for transfers between devices: 73.3 us -> none  [body(): lax.all_gather(w_hidden, POOL, axis=0, tiled=True)]
    pallas_call x0 -> x1, Pallas kernels: none -> 42.1 us  [tower(): pl.pallas_call(tower_kernel, out_shape=jax.ShapeDtypeStruct((M, E), jnp.f...]
    dot_general x1 -> x0, matrix products: 16.4 us -> none  [body(): partial_value = jnp.dot(hidden, w_out, preferred_element_type=jnp.float32)]
  transfers between devices with their start and end apart: 5 -> 4, of which waited for: 1 -> 0; matrix products, arithmetic and copies ran while one was open for 18% -> 22% of each run, Pallas kernels for 0% -> 0%
where the time goes in v1:
time: 233 us; the launch traced here: 231 us
  blocking collectives  86.9 us (37%)
  Pallas kernels  42.1 us (18%)
  starting transfers between devices  27.1 us (12%)
  other arithmetic  21.5 us (9%)
  local copies, waits for them, and re-layouts  18.7 us (8%)
  matrix products  18.5 us (8%)
  between operations  15 us (6%)
    pallas_call x1, Pallas kernels, tower(): pl.pallas_call(tower_kernel, out_shape=jax.ShapeDtypeStruct((M, E), jnp.f...  42.1 us
    all_gather x1, blocking collectives, body(): target_piece = lax.all_gather(positives, POOL, axis=0, tiled=True)  36.2 us
    all_gather x3, blocking collectives, all_in_one(): both, at, found = (lax.all_gather(jnp.concatenate(lines), axis), 0, {})  30.1 us
    all_to_all x1, blocking collectives, sum_at_owner(): blocks = lax.all_to_all(split_up(x, dim, count), axis, 0, 0, tiled=True)  20.6 us
    dot_general x2, matrix products, block_step(): jnp.dot(query_rows, bank_block.T, preferred_element_type=jnp.float32)  18.5 us
    reduce_sum x2, other arithmetic, block_step(): jnp.sum(jnp.where(columns[None, :] == target_rows[:, None], logits, 0.0),...  16.2 us
    all_to_all x1, starting transfers between devices, body(): lax.all_to_all(rows_out.reshape(peer_count, capacity, -1), POOL, split_ax...  11.1 us
    all_to_all x1, starting transfers between devices, copy_for_each(): return lax.all_to_all(copies, axis, split_axis=0, concat_axis=0, tiled=True)  8.33 us
  transfers between devices with their start and end apart: 4, of which 0 were waited for; matrix products, arithmetic and copies ran while one was open for 22% of the time, Pallas kernels for 0%

profile of v1, /device:TPU:2, one launch (start us, length us, event | category | flops | bytes accessed | tf_op | source)
XLA Modules:
  0.0 231.2 jit_solution(4094824420969664554)
XLA Ops:
  7.3 1.1 copy-done.1
  8.4 0.9 copy-done.2
  9.4 42.1 %tower.1 = f32[1024,256]{1,0:T(8,128)S(1)} custom-call(bf16[1,1024,4096]{2,1,0:T(8,128)(2,1)} %tok_hbm.1, bf16[128,1024]{1,0:T(8,128)(2,1)S(1)} %copy-done.2, bf16[1024,256]{1,0:T(8,128)(2,1)S(1)} %copy-done.1), custom_call_target="tpu_custom_call" | custom-call | tf_op jit(solution)/shard_map/tower/pallas_call | solution.py:321
  51.5 20.6 %all_to_all.28 = f32[4,256,256]{2,1,0:T(8,128)} all-to-all(f32[4,256,256]{2,1,0:T(8,128)S(1)} %bitcast.230), channel_id=1, replica_groups=mesh['dp'=2,'tensor'=4,'pool_0'=4,'pool_1'=4,'pool_2'=2] {'tensor'}, dimensions={0} | all-to-all | bytes 2097152 | tf_op jit(solution)/shard_map/all_to_all | solution.py:28
  72.0 2.0 reduce_sum.56
  74.0 0.8 convert_reduce_fusion
  74.8 0.6 broadcast_in_dim.52
  75.5 8.3 %all-to-all-start.1 = ((s32[32,1,32]{2,1,0:T(1,128)}), s32[32,1,32]{2,1,0:T(1,128)S(1)}, u32[]{:S(2)}, u32[]{:S(2)}) async-start(s32[32,1,32]{2,1,0:T(1,128)} %broadcast_in_dim.52), calls=%async_computation.1 | async-start | bytes 32768 | tf_op jit(solution)/shard_map/all_to_all | solution.py:60
  83.8 0.7 fusion.38
  84.5 6.8 %gather_fusion = bf16[1024]{0:T(1024)(128)(2,1)S(1)} fusion(bf16[1048576]{0:T(1024)(128)(2,1)S(1)} %copy-done, s32[1024]{0:T(1024)S(1)} %fusion.38), kind=kCustom, calls=%fused_computation | custom fusion | bytes 8192 | tf_op jit(solution)/shard_map/jit(_take)/gather | solution.py:347
  91.3 0.6 reduce-window.6
  91.9 0.2 slice_reduce_fusion
  92.5 0.1 select_reduce_fusion
  92.6 1.4 scatter_custom_fusion
  94.0 0.7 all_to_all.21
  94.7 7.7 %all-to-all-start.2 = ((s32[32,1,16]{2,1,0:T(1,128)}), s32[32,1,16]{2,1,0:T(1,128)S(1)}, u32[]{:S(2)}, u32[]{:S(2)}) async-start(s32[32,1,16]{2,1,0:T(1,128)} %bitcast.36), calls=%async_computation.2 | async-start | bytes 32768 | tf_op jit(solution)/shard_map/all_to_all | solution.py:397
  102.4 36.2 %all-gather.4 = s32[32,1,256]{2,1,0:T(1,128)S(1)} all-gather(s32[1,1,256]{2,1,0:T(1,128)S(1)} %bitcast.250), channel_id=1, replica_groups=mesh['dp'=2,'tensor'=4,'pool_0'=4,'pool_1'=4,'pool_2'=2] {'pool_0','pool..., dimensions={0}, use_global_device_ids=true | all-gather | bytes 33792 | tf_op jit(solution)/shard_map/all_gather | solution.py:351
  139.3 2.5 %scatter_custom_fusion.1 = bf16[512,256]{1,0:T(8,128)(2,1)} fusion(s32[256]{0:T(256)S(1)} %bitcast.252, bf16[256,256]{1,0:T(8,128)(2,1)} %param.19, bf16[]{:T(256)} %constant.89.clone.1), kind=kCustom, calls=%fused_computation.19 | custom fusion | bytes 262656 | tf_op jit(solution)/shard_map/scatter | solution.py:386
  141.8 11.1 %all-to-all-start.3 = ((bf16[32,16,256]{2,1,0:T(8,128)(2,1)}), bf16[32,16,256]{2,1,0:T(8,128)(2,1)S(1)}, u32[]{:S(2)}, u32[]{:S(2)}) async-start(bf16[32,16,256]{2,1,0:T(8,128)(2,1)} %bitcast.39), calls=%async_computation.3 | async-start | bytes 524288 | tf_op jit(solution)/shard_map/all_to_all | solution.py:390
  153.2 37.4 %while.15 = (s32[]{:T(128)}, f32[8192]{0:T(1024)S(1)}, f32[8192]{0:T(1024)S(1)}, f32[8192]{0:T(1024)S(1)}, bf16[2,512,256]{2,1,0:T(8,128)(2,1)S(1)}, /*index=5*/...) while((s32[]{:T(128)}, f32[8192]{0:T(1024)S(1)}, ...), condition=%wide.region_5.6_spmd.clone, body=%wide.region_1.5_spmd.clone.sunk | while | flops 2181087744 | bytes 38676668 | solution.py:113
  153.3 9.2 %fusion.63 = (f32[8192]{0:T(1024)S(1)}, f32[512,8192]{1,0:T(8,128)}) fusion(f32[512]{0:T(512)S(1)} %bitcast.233, bf16[8192,256]{1,0:T(8,128)(2,1)} %get-tuple-element.234, bf16[2,512,256]{2,1,0:T(8,128)(2,1)S(1)} %get-tuple-element.233, s32[]{:T(128)S(6)} %copy.27), kind=kOutput, calls=%fused_computation.124.clone.1 | convolution fusion | flops 2160058368 | bytes 21268484 | tf_op jit(solution)/shard_map/while/body/eval_jaxpr/dot_general | solution.py:95
  162.5 0.6 dynamic_slice.94
  163.8 8.1 %fusion.64 = (f32[8192]{0:T(1024)S(1)}, f32[8192]{0:T(1024)S(1)}) fusion(f32[512,8192]{1,0:T(8,128)} %get-tuple-element.198, s32[8192]{0:T(1024)S(1)} %bitcast.234, s32[512]{0:T(512)S(1)} %iota_add_fusion.2, f32[8192]{0:T(1024)S(1)} %select_maximum_fusion.2), kind=kLoop, calls=%fused_computation.8.clone.1 | loop fusion | flops 20955136 | bytes 16910336 | tf_op jit(solution)/shard_map/while/body/eval_jaxpr/reduce_sum | solution.py:103
  171.9 9.2 %fusion.63 = (f32[8192]{0:T(1024)S(1)}, f32[512,8192]{1,0:T(8,128)}) fusion(f32[512]{0:T(512)S(1)} %bitcast.233, bf16[8192,256]{1,0:T(8,128)(2,1)} %get-tuple-element.234, bf16[2,512,256]{2,1,0:T(8,128)(2,1)S(1)} %get-tuple-element.233, s32[]{:T(128)S(6)} %copy.27), kind=kOutput, calls=%fused_computation.124.clone.1 | convolution fusion | flops 2160058368 | bytes 21268484 | tf_op jit(solution)/shard_map/while/body/eval_jaxpr/dot_general | solution.py:95
  181.2 0.6 dynamic_slice.94
  182.4 8.1 %fusion.64 = (f32[8192]{0:T(1024)S(1)}, f32[8192]{0:T(1024)S(1)}) fusion(f32[512,8192]{1,0:T(8,128)} %get-tuple-element.198, s32[8192]{0:T(1024)S(1)} %bitcast.234, s32[512]{0:T(512)S(1)} %iota_add_fusion.2, f32[8192]{0:T(1024)S(1)} %select_maximum_fusion.2), kind=kLoop, calls=%fused_computation.8.clone.1 | loop fusion | flops 20955136 | bytes 16910336 | tf_op jit(solution)/shard_map/while/body/eval_jaxpr/reduce_sum | solution.py:103
  190.7 13.1 %all-gather.1 = f32[384,256]{1,0:T(8,128)S(1)} all-gather(f32[96,256]{1,0:T(8,128)S(1)} %pad_maximum_fusion), channel_id=3, replica_groups=mesh['dp'=2,'tensor'=4,'pool_0'=4,'pool_1'=4,'pool_2'=2] {'pool_0'}, dimensions={0}, use_global_device_ids=true | all-gather | bytes 491520 | tf_op jit(solution)/shard_map/all_gather | solution.py:40
  203.8 15.1 %all-gather.2 = f32[384,256]{1,0:T(8,128)S(1)} all-gather(f32[96,256]{1,0:T(8,128)S(1)} %pad_maximum_fusion.1), channel_id=4, replica_groups=mesh['dp'=2,'tensor'=4,'pool_0'=4,'pool_1'=4,'pool_2'=2] {'pool_1'}, dimensions={0}, use_global_device_ids=true | all-gather | bytes 491520 | tf_op jit(solution)/shard_map/all_gather | solution.py:40
  219.0 1.9 all-gather.3
  221.0 2.6 %scatter_fusion = bf16[1024,256]{1,0:T(8,128)(2,1)S(1)} fusion(bf16[1024,256]{1,0:T(8,128)(2,1)S(1)} %bitcast.231, s32[512]{0:T(512)S(1)} %bitcast.249, bf16[512,256]{1,0:T(8,128)(2,1)S(1)} %bitcast.243), kind=kCustom, calls=%fused_computation.3 | custom fusion | bytes 788480 | tf_op jit(solution)/shard_map/scatter | solution.py:404
  223.6 0.7 fusion.46
  224.3 0.1 copy-done.3
  (75 shorter events, 1.1 us)
Async XLA Ops:
  7.2 77.3 %copy-start = (bf16[1048576]{0:T(1024)(128)(2,1)S(1)}, bf16[1048576]{0:T(1024)(128)(2,1)}, u32[]{:S(2)}) copy-start(bf16[1048576]{0:T(1024)(128)(2,1)} %param.17) | copy-start | bytes 6291460
  7.2 146.0 %copy-start.4 = (bf16[1024,256]{1,0:T(8,128)(2,1)S(1)}, bf16[1024,256]{1,0:T(8,128)(2,1)}, u32[]{:S(2)}) copy-start(bf16[1024,256]{1,0:T(8,128)(2,1)} %param.15) | copy-start | bytes 1572868
  7.2 84.9 %copy-start.5 = (s32[1024]{0:T(1024)S(1)}, s32[1024]{0:T(1024)}, u32[]{:S(2)}) copy-start(s32[1024]{0:T(1024)} %param.16) | copy-start | bytes 12292
  7.2 95.2 %copy-start.7 = (s32[1,256]{1,0:T(1,128)S(1)}, s32[1,256]{1,0:T(1,128)}, u32[]{:S(2)}) copy-start(s32[1,256]{1,0:T(1,128)} %param.18) | copy-start | bytes 3076
  7.2 84.1 %copy-start.6 = (s32[256,1]{0,1:T(1,128)S(1)}, s32[256,1]{0,1:T(1,128)}, u32[]{:S(2)}) copy-start(s32[256,1]{0,1:T(1,128)} %param.20) | copy-start | bytes 3076
  7.2 146.0 %all-gather.7.cloned.1.call-start = ((), (), s32[]{:S(2)}) async-start(), calls=%async_computation.4 | async-start | bytes 4325376 | tf_op jit(solution)/shard_map/all_gather | solution.py:350
  7.3 1.2 copy-start.1
  8.4 0.9 copy-start.2
  75.5 16.7 %all-to-all-start.1 = ((s32[32,1,32]{2,1,0:T(1,128)}), s32[32,1,32]{2,1,0:T(1,128)S(1)}, u32[]{:S(2)}, u32[]{:S(2)}) async-start(s32[32,1,32]{2,1,0:T(1,128)} %broadcast_in_dim.52), calls=%async_computation.1 | async-start | bytes 32768 | tf_op jit(solution)/shard_map/all_to_all | solution.py:60
  94.7 47.1 %all-to-all-start.2 = ((s32[32,1,16]{2,1,0:T(1,128)}), s32[32,1,16]{2,1,0:T(1,128)S(1)}, u32[]{:S(2)}, u32[]{:S(2)}) async-start(s32[32,1,16]{2,1,0:T(1,128)} %bitcast.36), calls=%async_computation.2 | async-start | bytes 32768 | tf_op jit(solution)/shard_map/all_to_all | solution.py:397
  141.8 79.2 %all-to-all-start.3 = ((bf16[32,16,256]{2,1,0:T(8,128)(2,1)}), bf16[32,16,256]{2,1,0:T(8,128)(2,1)S(1)}, u32[]{:S(2)}, u32[]{:S(2)}) async-start(bf16[32,16,256]{2,1,0:T(8,128)(2,1)} %bitcast.39), calls=%async_computation.3 | async-start | bytes 524288 | tf_op jit(solution)/shard_map/all_to_all | solution.py:390
  223.6 0.8 copy-start.3
Sparse Core Ops, SparseCore 0:
  74.2 60.6 all-gather.6

commit v2 on v1

--- a/solution.py
+++ b/solution.py
@@ -10,126 +10,19 @@
 from jax.sharding import PartitionSpec as P
 
 MESH = pl.DeviceIdType.MESH
-
 POOL = ("pool_0", "pool_1", "pool_2")
 DP_POOL = ("dp", "pool_0", "pool_1", "pool_2")
 
 
-inv_temp = 5.0
-
-
-def split_up(x, dim, count):
-    before, after = (x.shape[:dim], x.shape[dim + 1 :])
-    return jnp.moveaxis(x.reshape(*before, count, -1, *after), dim, 0)
-
-
-def sum_at_owner(x, axis, dim):
-    count = lax.axis_size(axis)
-    blocks = lax.all_to_all(split_up(x, dim, count), axis, 0, 0, tiled=True)
-    return jnp.sum(blocks, axis=0)
-
-
-def all_in_one(x, axis):
-    leaves = jax.tree.leaves(x)
-    turns = sorted(range(len(leaves)), key=lambda k: -leaves[k].size)
-    width = (1, *leaves[turns[0]].shape)[-1]
-    lines = [
-        jnp.pad(leaves[k].reshape(-1), (0, -leaves[k].size % width)).reshape(-1, width)
-        for k in turns
-    ]
-    both, at, found = (lax.all_gather(jnp.concatenate(lines), axis), 0, {})
-    for k, line in zip(turns, lines):
-        section = both[:, at : at + len(line)].reshape(len(both), -1)
-        found[k] = section[:, : leaves[k].size].reshape(-1, *leaves[k].shape)
-        at += len(line)
-    numbers = iter(range(len(leaves)))
-    return jax.tree.map(lambda _: found[next(numbers)], x)
-
-
-def joined_all(x, axes, combine):
-    for axis in axes:
-        pieces = all_in_one(x, axis)
-        x = jax.tree.map(lambda part: part[0], pieces)
-        for k in range(1, lax.axis_size(axis)):
-            x = combine(x, jax.tree.map(lambda part: part[k], pieces))
-    return x
-
-
-def copy_for_each(x, axis):
-    copies = jnp.broadcast_to(x, (lax.axis_size(axis), *x.shape))
-    return lax.all_to_all(copies, axis, split_axis=0, concat_axis=0, tiled=True)
-
-
-def folded_in_pairs(pieces, combine):
-    while len(jax.tree.leaves(pieces)[0]) > 1:
-        pieces = jax.vmap(combine)(*(pieces[side::2] for side in (0, 1)))
-    return pieces[0]
-
-
-def entering(x, axis, combine, identity):
-    count, position = (lax.axis_size(axis), lax.axis_index(axis))
-    passed = jnp.arange(count) < position
-
-    def kept(part, zero, own):
-        part = jnp.where(
-            passed.reshape(-1, *(1 for _ in own.shape)), part, jnp.asarray(zero, own.dtype)
-        )
-        return part
-
-    pieces = copy_for_each(x, axis)
-    return folded_in_pairs(kept(pieces, identity, x), combine)
-
-
-def local_stats(query_rows, target_rows, bank, offsets, base_column):
-    row_count = query_rows.shape[0]
-    bank_rows = bank.shape[0]
-    block_width = 512
-    block_count = bank_rows // block_width
-    blocks = bank.reshape(block_count, block_width, bank.shape[1])
-    shifts = offsets.reshape(block_count, block_width)
-
-    def block_step(running, inputs):
-        run_max, run_sum, run_pos = running
-        bank_block, block_offsets, block_index = inputs
-        logits = (
-            inv_temp * jnp.dot(query_rows, bank_block.T, preferred_element_type=jnp.float32)
-            - block_offsets[None, :]
-        )
-        next_max = jnp.maximum(run_max, jnp.max(logits, axis=1))
-        run_sum = run_sum * jnp.exp(run_max - next_max) + jnp.sum(
-            jnp.exp(logits - next_max[:, None]), axis=1
-        )
-        columns = base_column + block_index * block_width + jnp.arange(block_width, dtype=jnp.int32)
-        run_pos = run_pos + jnp.sum(
-            jnp.where(columns[None, :] == target_rows[:, None], logits, 0.0), axis=1
-        )
-        return ((next_max, run_sum, run_pos), None)
-
-    initial = (
-        jnp.full((row_count,), -jnp.inf, jnp.float32),
-        jnp.zeros((row_count,), jnp.float32),
-        jnp.zeros((row_count,), jnp.float32),
-    )
-    final, _ = lax.scan(
-        block_step, initial, (blocks, shifts, jnp.arange(block_count, dtype=jnp.int32))
-    )
-    return final
-
-
-def combine(earlier_part, later_part):
-    both_max = jnp.maximum(earlier_part[0], later_part[0])
-    both_sum = earlier_part[1] * jnp.exp(earlier_part[0] - both_max) + later_part[1] * jnp.exp(
-        later_part[0] - both_max
-    )
-    return (both_max, both_sum, earlier_part[2] + later_part[2])
-
-
-def add_counts(earlier_part, later_part):
-    return earlier_part + later_part
-
-
-def tower_kernel(tok_hbm, w_hbm, wo_ref, out_ref, tok, wbuf, acc, tok_sem, own_sem, send_sem, recv_sem, psend, precv):
+LOG2E = 1.4426950408889634
+LN2 = 0.6931471805599453
+
+
+def tower_kernel(tok_hbm, w_hbm, wo_ref, bank_hbm, off_hbm, pos_ref, out_ref, tok, wbuf, acc, part, ysend, yrecv,
+                 bankbuf, offb, qbuf, qt, tbuf, sbuf, stats, tok_sem, own_sem, send_sem, recv_sem, psend, precv,
+                 xsend, xrecv, ysem, yrsem, qsend, qrecv, tsend, trecv, ssend, srecv):
     dp, y, x, zl, c = (lax.axis_index(a) for a in AXES)
+    ny = lax.axis_size("tensor")
     pz = dp * 4 + zl
     R = w_hbm.shape[0]
     C = w_hbm.shape[1] // 2
@@ -146,6 +39,9 @@
         return chip(step, 0) if (h == 0) == first else chip(0, step)
 
     partner = (dp, y, x, zl, 1 - c)
+
+    def column(step):
+        return (dp, lax.rem(y + step + ny, ny), x, zl, c)
 
     def block_of(h, f, s):
         dx = f * (1 - h) + s * h
@@ -197,12 +93,18 @@
     def pieces(f, s):
         return (0, 1) if (f == 2 and s == 0) or s == 2 else (None,)
 
+    B = bank_hbm.shape[0]
+    mine = pl.ds(pl.multiple_of(c * B, B), B)
     own = [pltpu.make_async_copy(w_hbm.at[:, pl.ds(h * C, C)], view(h, 0, 0, None, c), own_sem.at[h]) for h in (0, 1)]
+    own.append(pltpu.make_async_copy(bank_hbm, bankbuf.at[mine, :], own_sem.at[2]))
+    own.append(pltpu.make_async_copy(off_hbm, offb.at[mine, :], own_sem.at[3]))
     for cp in own:
         cp.start()
 
     barrier = pltpu.get_barrier_semaphore()
     peers = [chip(1, 0), chip(-1, 0), chip(0, 1), chip(0, -1), partner]
+    if ny > 1:
+        peers += [column(1), column(-1)]
     for p in peers:
         pl.semaphore_signal(barrier, inc=1, device_id=p, device_id_type=MESH)
 
@@ -236,6 +138,14 @@
     for h in (0, 1):
         for step in (1, -1):
             send(h, 0, 0, None, False, step, (0, -step))
+
+    swaps = []
+    for i, ref in enumerate((bankbuf, offb)):
+        cp = pltpu.make_async_remote_copy(
+            src_ref=ref.at[mine, :], dst_ref=ref.at[mine, :], send_sem=xsend.at[i], recv_sem=xrecv.at[i],
+            device_id=partner, device_id_type=MESH)
+        cp.start()
+        swaps.append(cp)
 
     def relay(g):
         for f, s in groups[g]:
@@ -296,76 +206,299 @@
     relay(8)
     mm(8)
 
-    T = min(256, M)
-
-    def out_step(r, carry):
-        rs = pl.ds(pl.multiple_of(r * T, T), T)
+    far = [(i, k) for i in offs for k in (0, -1, 1, 2, -2) if (i, k) != (0, 0)]
+
+    def spot(i, k):
+        return offs.index(i) * 5 + (0, -1, 1, 2, -2).index(k)
+
+    def mirror(i, k):
+        return spot(i if i == 2 else -i, -k)
+
+    tcopies = []
+    for n, (i, k) in enumerate(far):
+        cp = pltpu.make_async_remote_copy(
+            src_ref=pos_ref, dst_ref=tbuf.at[mirror(i, k)], send_sem=tsend.at[n], recv_sem=trecv.at[mirror(i, k)],
+            device_id=chip(i, k), device_id_type=MESH)
+        cp.start()
+        tcopies.append(cp)
+
+    T = M // 4
+    H = part.shape[1] // 2
+    left, right = pl.ds(0, H), pl.ds(H, H)
+
+    def quarter(step):
+        return pl.ds(pl.multiple_of(lax.rem(y + step + 4, 4) * T, T), T)
+
+    def partial(step):
+        rs = quarter(step)
         total = None
         for h in (0, 1):
             hid = jnp.maximum(acc[h, rs, :], 0.0).astype(jnp.bfloat16)
             d = jnp.dot(hid, wo_ref[pl.ds(h * C, C), :], preferred_element_type=jnp.float32)
             total = d if total is None else total + d
-        out_ref[rs, :] = total
-        return carry
-
-    lax.fori_loop(0, M // T, out_step, 0)
-
-    for cp in sends + psends:
+        part[rs, :] = total
+
+    ycopies = []
+
+    def ysend_to(slot, step):
+        cp = pltpu.make_async_remote_copy(
+            src_ref=ysend.at[slot], dst_ref=yrecv.at[slot], send_sem=ysem.at[slot], recv_sem=yrsem.at[slot],
+            device_id=column(step), device_id_type=MESH)
+        cp.start()
+        ycopies.append(cp)
+
+    def ywait(slot):
+        pltpu.make_async_remote_copy(
+            src_ref=ysend.at[slot], dst_ref=yrecv.at[slot], send_sem=ysem.at[slot], recv_sem=yrsem.at[slot],
+            device_id=partner, device_id_type=MESH).wait_recv()
+
+    bf = jnp.bfloat16
+    f32 = jnp.float32
+    if ny > 1:
+        partial(2)
+        ysend[0] = part[quarter(2), left].astype(bf)
+        ysend_to(0, -1)
+        ysend[1] = part[quarter(2), right].astype(bf)
+        ysend_to(1, 1)
+        partial(-1)
+        ysend[2] = part[quarter(-1), right].astype(bf)
+        ysend_to(2, -1)
+        partial(1)
+        ysend[3] = part[quarter(1), left].astype(bf)
+        ysend_to(3, 1)
+        ywait(0)
+        ysend[4] = (yrecv[0].astype(f32) + part[quarter(-1), left]).astype(bf)
+        ysend_to(4, -1)
+        ywait(1)
+        ysend[5] = (yrecv[1].astype(f32) + part[quarter(1), right]).astype(bf)
+        ysend_to(5, 1)
+        partial(0)
+        ywait(2)
+        ywait(3)
+        ywait(4)
+        ywait(5)
+        own_q = quarter(0)
+        qbuf[0, :, left] = (part[own_q, left] + yrecv[3].astype(f32) + yrecv[4].astype(f32)).astype(bf)
+        qbuf[0, :, right] = (part[own_q, right] + yrecv[2].astype(f32) + yrecv[5].astype(f32)).astype(bf)
+    else:
+        partial(0)
+        qbuf[0] = part[pl.ds(0, T), :].astype(bf)
+
+    P2 = T // 2
+    P4 = T // 4
+
+    def qview(h, f, s, piece):
+        dx, dz = (f, s) if h == 0 else (s, f)
+        rows = pl.ds(h * P2, P2) if piece is None else pl.ds(h * P2 + piece * P4, P4)
+        return qbuf.at[offs.index(dx) * 4 + offs.index(dz), rows, :]
+
+    qsends = []
+
+    def qgo(h, f, s, piece, first, step, kind):
+        cp = pltpu.make_async_remote_copy(
+            src_ref=qview(h, f, s, piece), dst_ref=qview(h, kind[0], kind[1], piece), send_sem=qsend.at[len(qsends)],
+            recv_sem=qrecv.at[key(h, kind[0], kind[1], piece)],
+            device_id=along(h, first, step), device_id_type=MESH)
+        cp.start()
+        qsends.append(cp)
+
+    def qwait(h, f, s, piece):
+        ref = qview(h, f, s, piece)
+        pltpu.make_async_remote_copy(
+            src_ref=ref, dst_ref=ref, send_sem=qsend.at[0],
+            recv_sem=qrecv.at[key(h, f, s, piece)], device_id=partner, device_id_type=MESH).wait_recv()
+
+    for first in (True, False):
+        for h in (0, 1):
+            for step in (1, -1):
+                qgo(h, 0, 0, None, first, step, (-step, 0) if first else (0, -step))
+
+    def qrelay(g):
+        for f, s in groups[g]:
+            for h in (0, 1):
+                for p in pieces(f, s):
+                    qwait(h, f, s, p)
+                if s == 0 and f != 2:
+                    qgo(h, f, 0, 0 if f == -1 else 1, True, -f, (2, 0))
+                if s == 0:
+                    for step in (1, -1):
+                        qgo(h, f, 0, None, False, step, (f, -step))
+                elif s != 2:
+                    qgo(h, f, s, 0 if s == -1 else 1, False, -s, (f, 2))
+
+    for cp in swaps:
+        cp.wait_recv()
+    tbuf[0] = pos_ref[...]
+    for i, k in far:
+        pltpu.make_async_remote_copy(
+            src_ref=pos_ref, dst_ref=tbuf.at[spot(i, k)], send_sem=tsend.at[0], recv_sem=trecv.at[spot(i, k)],
+            device_id=partner, device_id_type=MESH).wait_recv()
+
+    base = (x * 4 + zl) * (2 * B)
+    CH = min(512, 2 * B)
+    lane = lax.broadcasted_iota(jnp.int32, (1, T), 1)
+    lower = lax.rem(lane, P2) < P4
+    sub = lax.broadcasted_iota(jnp.int32, (8, T), 0)
+    W = sbuf.shape[2]
+    scopies = []
+
+    def block(dx, dz):
+        slot = offs.index(dx) * 4 + offs.index(dz)
+        qt[...] = jnp.transpose(qbuf[slot])
+        if dz == 2:
+            target = jnp.where(lower, tbuf[spot(dx, -2)], tbuf[spot(dx, 2)])
+        else:
+            target = tbuf[spot(dx, dz)]
+        t = jnp.broadcast_to(target - base, (8, T))
+        group = lax.shift_right_arithmetic(t, 3)
+
+        def chunk(k, carry):
+            m, total, hit = carry
+            rows = pl.ds(pl.multiple_of(k * CH, CH), CH)
+            prod = jnp.dot(bankbuf[rows, :], qt[...], preferred_element_type=f32)
+            off = offb[rows, :]
+            if T > off.shape[1]:
+                off = jnp.concatenate([off] * (T // off.shape[1]), axis=1)
+            logit = (prod * (5.0 * LOG2E) - off).reshape(CH // 8, 8, T)
+            top = jnp.maximum(m, jnp.max(logit, axis=0))
+            here = group - k * (CH // 8)
+            for r in range(CH // 8):
+                hit = jnp.where(here == r, logit[r], hit)
+            total = total * jnp.exp2(m - top) + jnp.sum(jnp.exp2(logit - top[None]), axis=0)
+            return top, total, hit
+
+        zero = jnp.zeros((8, T), f32)
+        m, total, hit = lax.fori_loop(0, 2 * B // CH, chunk, (jnp.full((8, T), -jnp.inf, f32), zero, zero))
+        top = jnp.max(m, axis=0, keepdims=True)
+        total = jnp.sum(total * jnp.exp2(m - top), axis=0, keepdims=True)
+        score = jnp.sum(jnp.where(jnp.bitwise_and(t, 7) == sub, hit, 0.0), axis=0, keepdims=True)
+        for n, v in enumerate((top, total, score)):
+            for k in range(2):
+                sbuf[slot, pl.ds(n * 2 + k, 1), :] = v[:, k * W:(k + 1) * W]
+        for k in ((dz,) if dz != 2 else (2, -2)):
+            if (dx, k) == (0, 0):
+                continue
+            cp = pltpu.make_async_remote_copy(
+                src_ref=sbuf.at[slot], dst_ref=stats.at[mirror(dx, k)], send_sem=ssend.at[len(scopies)],
+                recv_sem=srecv.at[mirror(dx, k)], device_id=chip(dx, k), device_id_type=MESH)
+            cp.start()
+            scopies.append(cp)
+
+    block(0, 0)
+    qrelay(1)
+    qrelay(2)
+    for dx, dz in ((-1, 0), (1, 0), (0, -1), (0, 1)):
+        block(dx, dz)
+    qrelay(3)
+    qrelay(4)
+    for dx, dz in ((-1, -1), (-1, 1), (1, -1), (1, 1)):
+        block(dx, dz)
+    qrelay(5)
+    block(2, 0)
+    block(0, 2)
+    qrelay(6)
+    qrelay(7)
+    for dx, dz in ((2, -1), (2, 1), (-1, 2), (1, 2)):
+        block(dx, dz)
+    qrelay(8)
+    block(2, 2)
+
+    stats[0] = sbuf[0]
+    for i, k in far:
+        pltpu.make_async_remote_copy(
+            src_ref=sbuf.at[0], dst_ref=stats.at[spot(i, k)], send_sem=ssend.at[0], recv_sem=srecv.at[spot(i, k)],
+            device_id=partner, device_id_type=MESH).wait_recv()
+    low = lax.broadcasted_iota(jnp.int32, (8, W), 1) < P4
+    parts = []
+    for i in offs:
+        for k in (0, -1, 1):
+            st = stats[spot(i, k)]
+            parts.append((st[0:2], st[2:4], st[4:6]))
+        st = jnp.where(low, stats[spot(i, 2)], stats[spot(i, -2)])
+        parts.append((st[0:2], st[2:4], st[4:6]))
+    top = functools.reduce(jnp.maximum, [p[0] for p in parts])
+    total = sum(p[1] * jnp.exp2(p[0] - top) for p in parts)
+    score = sum(p[2] for p in parts)
+    loss = LN2 * (top - score) + jnp.log(total)
+    for k in range(2):
+        out_ref[:, k * W:(k + 1) * W] = loss[k:k + 1, :]
+
+    for cp in sends + psends + swaps + tcopies + ycopies + qsends + scopies:
         cp.wait_send()
 
 
-def tower(tokens, w_hidden, w_out):
+def tower(tokens, w_hidden, w_out, bank, offsets, positives):
     M, K = tokens.shape[1:]
     R, N = w_hidden.shape
     E = w_out.shape[1]
+    B = bank.shape[0]
+    T = M // 4
+    anywhere = pl.BlockSpec(memory_space=pl.ANY)
+    vmem = pl.BlockSpec(memory_space=pltpu.VMEM)
+    dma = pltpu.SemaphoreType.DMA
     return pl.pallas_call(
         tower_kernel,
-        out_shape=jax.ShapeDtypeStruct((M, E), jnp.float32),
-        in_specs=[pl.BlockSpec(memory_space=pl.ANY), pl.BlockSpec(memory_space=pl.ANY), pl.BlockSpec(memory_space=pltpu.VMEM)],
-        out_specs=pl.BlockSpec(memory_space=pltpu.VMEM),
+        out_shape=jax.ShapeDtypeStruct((1, T), jnp.float32),
+        in_specs=[anywhere, anywhere, vmem, anywhere, anywhere, vmem],
+        out_specs=vmem,
         scratch_shapes=[
             pltpu.VMEM((16, M, 2 * R), jnp.bfloat16),
             pltpu.VMEM((2, K, N // 2), jnp.bfloat16),
             pltpu.VMEM((2, M, N // 2), jnp.float32),
-            pltpu.SemaphoreType.DMA((16,)),
-            pltpu.SemaphoreType.DMA((2,)),
-            pltpu.SemaphoreType.DMA((46,)),
-            pltpu.SemaphoreType.DMA((64,)),
-            pltpu.SemaphoreType.DMA((64,)),
-            pltpu.SemaphoreType.DMA((64,)),
+            pltpu.VMEM((M, E), jnp.float32),
+            pltpu.VMEM((6, T, E // 2), jnp.bfloat16),
+            pltpu.VMEM((6, T, E // 2), jnp.bfloat16),
+            pltpu.VMEM((2 * B, E), jnp.bfloat16),
+            pltpu.VMEM((2 * B, offsets.shape[1]), jnp.float32),
+            pltpu.VMEM((16, T, E), jnp.bfloat16),
+            pltpu.VMEM((E, T), jnp.bfloat16),
+            pltpu.VMEM((20, 1, T), jnp.int32),
+            pltpu.VMEM((16, 8, T // 2), jnp.float32),
+            pltpu.VMEM((20, 8, T // 2), jnp.float32),
+            dma((16,)), dma((4,)), dma((40,)), dma((64,)), dma((64,)), dma((64,)),
+            dma((2,)), dma((2,)), dma((6,)), dma((6,)), dma((40,)), dma((64,)),
+            dma((19,)), dma((20,)), dma((19,)), dma((20,)),
         ],
-        compiler_params=pltpu.CompilerParams(collective_id=0, has_side_effects=True, vmem_limit_bytes=50 * 1024 * 1024),
+        compiler_params=pltpu.CompilerParams(collective_id=0, has_side_effects=True, vmem_limit_bytes=56 * 1024 * 1024),
         name="tower",
-    )(tokens, w_hidden, w_out)
+    )(tokens, w_hidden, w_out, bank, offsets, positives)
+
+
+def copy_for_each(x, axis):
+    copies = jnp.broadcast_to(x, (lax.axis_size(axis), *x.shape))
+    return lax.all_to_all(copies, axis, split_axis=0, concat_axis=0, tiled=True)
+
+
+def folded_in_pairs(pieces, combine):
+    while len(jax.tree.leaves(pieces)[0]) > 1:
+        pieces = jax.vmap(combine)(*(pieces[side::2] for side in (0, 1)))
+    return pieces[0]
+
+
+def entering(x, axis, combine, identity):
+    count, position = (lax.axis_size(axis), lax.axis_index(axis))
+    passed = jnp.arange(count) < position
+
+    def kept(part, zero, own):
+        part = jnp.where(
+            passed.reshape(-1, *(1 for _ in own.shape)), part, jnp.asarray(zero, own.dtype)
+        )
+        return part
+
+    pieces = copy_for_each(x, axis)
+    return folded_in_pairs(kept(pieces, identity, x), combine)
+
+
+def add_counts(earlier_part, later_part):
+    return earlier_part + later_part
 
 
 def body(
     tokens, w_hidden, w_out, bank, item_ids, log_freq, positives, new_items, new_owner, queue_head
 ):
-    partial_value = tower(tokens, w_hidden, w_out)
-    queries = sum_at_owner(partial_value, "tensor", 0).astype(jnp.bfloat16)
-    offsets = jnp.take(log_freq, item_ids).astype(jnp.float32)
-    own_index = lax.axis_index(POOL)
-    base_column = own_index * bank.shape[0]
-    query_piece = lax.all_gather(queries[None], POOL, axis=0, tiled=True)
-    target_piece = lax.all_gather(positives, POOL, axis=0, tiled=True)
-    groups_in = query_piece.shape[0]
-    run_max, run_sum, run_pos = local_stats(
-        query_piece.reshape(-1, query_piece.shape[2]),
-        target_piece.reshape(-1),
-        bank,
-        offsets,
-        base_column,
-    )
-    maxima = run_max.reshape(groups_in, -1)
-    totals = run_sum.reshape(groups_in, -1)
-    scores = run_pos.reshape(groups_in, -1)
-    maxima, totals, scores = (maxima, totals, scores)
-    maxima, totals, scores = joined_all((maxima, totals, scores), POOL, combine)
-    own_max = lax.dynamic_slice_in_dim(maxima, own_index, 1, 0)
-    own_sum = lax.dynamic_slice_in_dim(totals, own_index, 1, 0)
-    own_pos = lax.dynamic_slice_in_dim(scores, own_index, 1, 0)
-    query_loss = own_max + jnp.log(own_sum) - own_pos
+    offsets = jnp.take(log_freq, item_ids).astype(jnp.float32) * LOG2E
+    offsets = jnp.broadcast_to(offsets[:, None], (bank.shape[0], 128))
+    query_loss = tower(tokens, w_hidden, w_out, bank, offsets, positives)
     owners = new_owner[:, 0]
     head_slot = queue_head[0]
     shard_rows = bank.shape[0]

time: 233 us -> 142 us (0.61)
  blocking collectives: 86.9 us -> 0 us
  Pallas kernels: 42.1 us -> 89.6 us
  matrix products: 18.5 us -> 0 us
  other arithmetic: 21.5 us -> 4.49 us
  between operations: 15 us -> 1.47 us
  starting transfers between devices: 27.1 us -> 21.8 us
  waiting for transfers between devices: 0.04 us -> 5.04 us
    all_gather x4 -> x0, blocking collectives: 66.3 us -> none  [the longest x1 36.2 us: body(): target_piece = lax.all_gather(positives, POOL, axis=0, tiled=True)]
    pallas_call x1, Pallas kernels: 42.1 us -> 89.6 us  [tower(): pl.pallas_call(tower_kernel, out_shape=jax.ShapeDtypeStruct((1, T), jnp.f...]
    all_to_all x1 -> x0, blocking collectives: 20.6 us -> none  [sum_at_owner(): blocks = lax.all_to_all(split_up(x, dim, count), axis, 0, 0, tiled=True)]
    dot_general x2 -> x0, matrix products: 18.5 us -> none  [block_step(): jnp.dot(query_rows, bank_block.T, preferred_element_type=jnp.float32)]
    reduce_sum x3 -> x0, other arithmetic: 18.2 us -> none  [the longest x2 16.2 us: block_step(): jnp.sum(jnp.where(columns[None, :] == target_rows[:, None], logits, 0.0),...]
    all_to_all x1, waiting for transfers between devices: 0.01 us -> 5.04 us  [copy_for_each(): return lax.all_to_all(copies, axis, split_axis=0, concat_axis=0, tiled=True)]
    all_to_all x1, starting transfers between devices: 11.1 us -> 7.77 us  [body(): lax.all_to_all(rows_out.reshape(peer_count, capacity, -1), POOL, split_ax...]
    all_to_all x1, starting transfers between devices: 7.69 us -> 4.97 us  [body(): lax.all_to_all(ranks_out.reshape(peer_count, capacity), POOL, split_axis=...]
  transfers between devices with their start and end apart: 4 -> 3, of which waited for: 0 -> 1; matrix products, arithmetic and copies ran while one was open for 22% -> 9% of each run, Pallas kernels for 0% -> 63%
where the time goes in v2:
time: 142 us; the launch traced here: 141 us
  Pallas kernels  89.6 us (63%)
  starting transfers between devices  21.8 us (15%)
  local copies, waits for them, and re-layouts  18.9 us (13%)
  waiting for transfers between devices  5.04 us (4%)
  other arithmetic  4.49 us (3%)
  between operations  1.47 us (1%)
    pallas_call x1, Pallas kernels, tower(): pl.pallas_call(tower_kernel, out_shape=jax.ShapeDtypeStruct((1, T), jnp.f...  89.6 us
    all_to_all x1, starting transfers between devices, copy_for_each(): return lax.all_to_all(copies, axis, split_axis=0, concat_axis=0, tiled=True)  9.05 us
    all_to_all x1, starting transfers between devices, body(): lax.all_to_all(rows_out.reshape(peer_count, capacity, -1), POOL, split_ax...  7.77 us
    gather x1, local copies, waits for them, and re-layouts, body(): offsets = jnp.take(log_freq, item_ids).astype(jnp.float32) * LOG2E  6.8 us
    all_to_all x1, waiting for transfers between devices, copy_for_each(): return lax.all_to_all(copies, axis, split_axis=0, concat_axis=0, tiled=True)  5.04 us
    all_to_all x1, starting transfers between devices, body(): lax.all_to_all(ranks_out.reshape(peer_count, capacity), POOL, split_axis=...  4.97 us
  transfers between devices with their start and end apart: 3, of which 1 were waited for; matrix products, arithmetic and copies ran while one was open for 9% of the time, Pallas kernels for 63%

profile of v2, /device:TPU:2, one launch (start us, length us, event | category | flops | bytes accessed | tf_op | source)
XLA Modules:
  0.0 141.3 jit_solution(3314957243066588943)
XLA Ops:
  0.6 0.0 copy-start
  0.6 0.0 copy-start.3
  0.7 2.0 %copy.21.bank_hbm = bf16[1024,256]{1,0:T(8,128)(2,1)} copy(bf16[1024,256]{1,0:T(8,128)(2,1)} %param.13) | data formatting | bytes 1048576
  2.7 0.8 convert_reduce_fusion
  3.5 0.6 broadcast_in_dim.47
  4.1 9.1 %all-to-all-start = ((s32[32,1,32]{2,1,0:T(1,128)}), s32[32,1,32]{2,1,0:T(1,128)S(1)}, u32[]{:S(2)}, u32[]{:S(2)}) async-start(s32[32,1,32]{2,1,0:T(1,128)} %broadcast_in_dim.47), calls=%async_computation | async-start | bytes 32768 | tf_op jit(solution)/shard_map/all_to_all | solution.py:469
  13.1 0.7 fusion.4
  13.8 0.6 reduce-window.6
  14.4 0.2 slice_reduce_fusion
  14.7 5.0 %all-to-all-done = s32[32,1,32]{2,1,0:T(1,128)S(1)} async-done(((s32[32,1,32]{2,1,0:T(1,128)}), s32[32,1,32]{2,1,0:T(1,128)S(1)}, u32[]{:S(2)}, u32[]{:S(2)}) %all-to-all-start) | async-done | bytes 4128 | tf_op jit(solution)/shard_map/all_to_all | solution.py:469
  19.7 0.1 broadcast_select_fusion
  20.0 0.8 select_reduce_fusion
  20.8 0.7 compare_select_fusion.4
  21.4 1.4 scatter_custom_fusion
  22.8 0.7 all_to_all.17
  23.5 5.0 %all-to-all-start.1 = ((s32[32,1,16]{2,1,0:T(1,128)}), s32[32,1,16]{2,1,0:T(1,128)S(1)}, u32[]{:S(2)}, u32[]{:S(2)}) async-start(s32[32,1,16]{2,1,0:T(1,128)} %bitcast.7), calls=%async_computation.1 | async-start | bytes 32768 | tf_op jit(solution)/shard_map/all_to_all | solution.py:530
  28.5 0.7 fusion.5
  29.2 6.8 %gather_fusion = bf16[1024]{0:T(1024)(128)(2,1)S(1)} fusion(bf16[1048576]{0:T(1024)(128)(2,1)S(1)} %copy-done, s32[1024]{0:T(1024)S(1)} %fusion.5), kind=kCustom, calls=%fused_computation | custom fusion | bytes 8192 | tf_op jit(solution)/shard_map/jit(_take)/gather | solution.py:499
  36.0 2.5 %scatter_custom_fusion.1 = bf16[512,256]{1,0:T(8,128)(2,1)} fusion(s32[256]{0:T(256)S(1)} %bitcast.35, bf16[256,256]{1,0:T(8,128)(2,1)} %param.17, bf16[]{:T(256)} %constant.65.clone.1), kind=kCustom, calls=%fused_computation.4 | custom fusion | bytes 262656 | tf_op jit(solution)/shard_map/scatter | solution.py:519
  38.5 0.0 all-to-all-done.1
  38.5 7.8 %all-to-all-start.2 = ((bf16[32,16,256]{2,1,0:T(8,128)(2,1)}), bf16[32,16,256]{2,1,0:T(8,128)(2,1)S(1)}, u32[]{:S(2)}, u32[]{:S(2)}) async-start(bf16[32,16,256]{2,1,0:T(8,128)(2,1)} %bitcast.10), calls=%async_computation.2 | async-start | bytes 524288 | tf_op jit(solution)/shard_map/all_to_all | solution.py:523
  46.3 0.0 copy-done.3
  47.0 1.0 broadcast_in_dim.44.off_hbm
  47.9 89.6 %tower.1 = f32[1,256]{1,0:T(1,128)} custom-call(bf16[1,1024,4096]{2,1,0:T(8,128)(2,1)} %tok_hbm.1, bf16[128,1024]{1,0:T(8,128)(2,1)} %w_hbm.1, bf16[1024,256]{1,0:T(8,128)(2,1)} %wo_ref.1, bf16[1024,256]{1,0:T(8,128)(2,1)} %copy.21.bank_hbm, f32[1024,128]{1,0:T(8,128)} %broadcast_in_dim.44.off_hbm, s32[1,256]{1,0:T(1,128)} %pos_ref.1), custom_call_target="tpu_custom_call" | custom-call | tf_op jit(solution)/shard_map/tower/pallas_call | solution.py:439
  137.5 0.1 compare_reduce_fusion
  137.6 0.1 ge.29
  137.7 0.1 add.97
  137.8 0.0 all-to-all-done.2
  137.9 2.6 %scatter_fusion = bf16[1024,256]{1,0:T(8,128)(2,1)S(1)} fusion(bf16[1024,256]{1,0:T(8,128)(2,1)S(1)} %copy-done.1, s32[512]{0:T(512)S(1)} %bitcast.33, bf16[512,256]{1,0:T(8,128)(2,1)S(1)} %bitcast.27), kind=kCustom, calls=%fused_computation.3 | custom fusion | bytes 788480 | tf_op jit(solution)/shard_map/scatter | solution.py:537
  140.5 0.0 copy-start.2
  140.5 0.6 copy.22
  141.1 0.2 copy-done.2
  (25 shorter events, 0.3 us)
Async XLA Ops:
  0.6 28.6 %copy-start = (bf16[1048576]{0:T(1024)(128)(2,1)S(1)}, bf16[1048576]{0:T(1024)(128)(2,1)}, u32[]{:S(2)}) copy-start(bf16[1048576]{0:T(1024)(128)(2,1)} %param.15) | copy-start | bytes 6291460
  0.6 45.6 %copy-start.3 = (s32[1024]{0:T(1024)S(1)}, s32[1024]{0:T(1024)}, u32[]{:S(2)}) copy-start(s32[1024]{0:T(1024)} %param.14) | copy-start | bytes 12292
  4.1 15.6 %all-to-all-start = ((s32[32,1,32]{2,1,0:T(1,128)}), s32[32,1,32]{2,1,0:T(1,128)S(1)}, u32[]{:S(2)}, u32[]{:S(2)}) async-start(s32[32,1,32]{2,1,0:T(1,128)} %broadcast_in_dim.47), calls=%async_computation | async-start | bytes 32768 | tf_op jit(solution)/shard_map/all_to_all | solution.py:469
  23.5 15.0 %all-to-all-start.1 = ((s32[32,1,16]{2,1,0:T(1,128)}), s32[32,1,16]{2,1,0:T(1,128)S(1)}, u32[]{:S(2)}, u32[]{:S(2)}) async-start(s32[32,1,16]{2,1,0:T(1,128)} %bitcast.7), calls=%async_computation.1 | async-start | bytes 32768 | tf_op jit(solution)/shard_map/all_to_all | solution.py:530
  38.5 99.3 %all-to-all-start.2 = ((bf16[32,16,256]{2,1,0:T(8,128)(2,1)}), bf16[32,16,256]{2,1,0:T(8,128)(2,1)S(1)}, u32[]{:S(2)}, u32[]{:S(2)}) async-start(bf16[32,16,256]{2,1,0:T(8,128)(2,1)} %bitcast.10), calls=%async_computation.2 | async-start | bytes 524288 | tf_op jit(solution)/shard_map/all_to_all | solution.py:523
  47.9 89.9 %copy-start.1 = (bf16[1024,256]{1,0:T(8,128)(2,1)S(1)}, bf16[1024,256]{1,0:T(8,128)(2,1)}, u32[]{:S(2)}) copy-start(bf16[1024,256]{1,0:T(8,128)(2,1)} %copy.21.bank_hbm) | copy-start | bytes 1572868
  137.9 2.6 %copy-start.4 = (f32[1,256]{1,0:T(1,128)S(1)}, f32[1,256]{1,0:T(1,128)}, u32[]{:S(2)}) copy-start(f32[1,256]{1,0:T(1,128)} %tower.1) | copy-start | bytes 3076
  140.5 0.8 copy-start.2

commit v3 on v2

--- a/solution.py
+++ b/solution.py
@@ -18,9 +18,11 @@
 LN2 = 0.6931471805599453
 
 
-def tower_kernel(tok_hbm, w_hbm, wo_ref, bank_hbm, off_hbm, pos_ref, out_ref, tok, wbuf, acc, part, ysend, yrecv,
-                 bankbuf, offb, qbuf, qt, tbuf, sbuf, stats, tok_sem, own_sem, send_sem, recv_sem, psend, precv,
-                 xsend, xrecv, ysem, yrsem, qsend, qrecv, tsend, trecv, ssend, srecv):
+def tower_kernel(tok_hbm, w_hbm, wo_ref, bank_hbm, freq_hbm, ids_ref, pos_ref, items_ref,
+                 owner_ref, head_ref, out_ref, newbank_ref, tok, wbuf, acc, part, ysend, yrecv,
+                 bankbuf, offb, qbuf, qt, tbuf, sbuf, stats, table, pick, where_at, found, packed, counts, rows_in, counts_in, tok_sem, own_sem, send_sem, recv_sem, psend, precv,
+                 xsend, xrecv, ysem, yrsem, qsend, qrecv, tsend, trecv, ssend, srecv,
+                 nsend, nrecv, csend, crecv):
     dp, y, x, zl, c = (lax.axis_index(a) for a in AXES)
     ny = lax.axis_size("tensor")
     pz = dp * 4 + zl
@@ -97,7 +99,7 @@
     mine = pl.ds(pl.multiple_of(c * B, B), B)
     own = [pltpu.make_async_copy(w_hbm.at[:, pl.ds(h * C, C)], view(h, 0, 0, None, c), own_sem.at[h]) for h in (0, 1)]
     own.append(pltpu.make_async_copy(bank_hbm, bankbuf.at[mine, :], own_sem.at[2]))
-    own.append(pltpu.make_async_copy(off_hbm, offb.at[mine, :], own_sem.at[3]))
+    freq_copy = pltpu.make_async_copy(freq_hbm, table, own_sem.at[3])
     for cp in own:
         cp.start()
 
@@ -140,12 +142,80 @@
             send(h, 0, 0, None, False, step, (0, -step))
 
     swaps = []
-    for i, ref in enumerate((bankbuf, offb)):
+
+    def swap(ref):
         cp = pltpu.make_async_remote_copy(
-            src_ref=ref.at[mine, :], dst_ref=ref.at[mine, :], send_sem=xsend.at[i], recv_sem=xrecv.at[i],
-            device_id=partner, device_id_type=MESH)
+            src_ref=ref.at[mine, :], dst_ref=ref.at[mine, :], send_sem=xsend.at[len(swaps)],
+            recv_sem=xrecv.at[len(swaps)], device_id=partner, device_id_type=MESH)
         cp.start()
         swaps.append(cp)
+
+    swap(bankbuf)
+    freq_copy.start()
+
+    bf = jnp.bfloat16
+    f32 = jnp.float32
+    i32 = jnp.int32
+
+    def onehot(a, b):
+        return jnp.where(a == b, 1.0, 0.0).astype(bf)
+
+    peers_in_pool = packed.shape[0]
+    cap = packed.shape[1]
+
+    def pack():
+        n = items_ref.shape[0]
+        width = counts.shape[1]
+        owner = owner_ref[...]
+        mark = jnp.where(lax.broadcasted_iota(i32, (width, n), 0) == owner, 1.0, 0.0)
+        lowrow = lax.broadcasted_iota(i32, (n, n), 0)
+        lowcol = lax.broadcasted_iota(i32, (n, n), 1)
+        upper = jnp.where(lowrow < lowcol, 1.0, 0.0).astype(bf)
+        ahead = jnp.dot(mark.astype(bf), upper, preferred_element_type=f32)
+        before = jnp.sum(mark * ahead, axis=0, keepdims=True)
+        place = owner * cap + before.astype(i32)
+        spread = onehot(lax.broadcasted_iota(i32, (peers_in_pool * cap, n), 0), place)
+        rows = jnp.dot(spread, items_ref[...], preferred_element_type=f32)
+        packed[...] = rows.astype(bf).reshape(packed.shape)
+        tally = lax.dot_general(jnp.ones((8, n), bf), mark.astype(bf), (((1,), (1,)), ((), ())), preferred_element_type=f32)
+        counts[...] = tally[0:1, :]
+
+    L = ids_ref.shape[1]
+    A = table.shape[0] // 8
+
+    def off_start():
+        for g in range(ids_ref.shape[0]):
+            row = ids_ref[g:g + 1, :].astype(f32)
+            idx = jnp.transpose(jnp.broadcast_to(row, (L, L))).astype(i32)
+            where_at[pl.ds(g * L, L), :] = idx
+            line = lax.rem(idx // L, A)
+            wide = jnp.concatenate([line] * (A // L), axis=1) if A > L else line[:, :A]
+            pick[pl.ds(g * L, L), :] = onehot(wide, lax.broadcasted_iota(i32, (L, A), 1))
+
+    def off_step(j):
+        if j == 0:
+            freq_copy.wait()
+        tile = min(256, B)
+
+        def rows_step(r, carry):
+            rs = pl.ds(pl.multiple_of(r * tile, tile), tile)
+            pair = jnp.concatenate([table[pl.ds(2 * j * A, A), :], table[pl.ds((2 * j + 1) * A, A), :]], axis=1)
+            d = jnp.dot(pick[rs, :], pair, preferred_element_type=f32)
+            part_of = where_at[rs, :] // (L * A)
+            got = jnp.where(part_of == 2 * j, d[:, :L], jnp.where(part_of == 2 * j + 1, d[:, L:], 0.0))
+            if j == 0:
+                found[rs, :] = got
+            else:
+                found[rs, :] = found[rs, :] + got
+            return carry
+
+        lax.fori_loop(0, B // tile, rows_step, 0)
+
+    def off_end():
+        lane_at = lax.broadcasted_iota(i32, (B, L), 1)
+        val = jnp.sum(jnp.where(lax.rem(where_at[...], L) == lane_at, found[...], 0.0), axis=1, keepdims=True)
+        offb[mine, :] = jnp.broadcast_to(val * LOG2E, (B, offb.shape[1]))
+        swap(offb)
 
     def relay(g):
         for f, s in groups[g]:
@@ -188,15 +258,22 @@
 
         lax.fori_loop(0, 2 * len(items), step, 0)
 
+    pack()
+    mm(0)
     relay(1)
-    mm(0)
+    off_start()
     relay(2)
     mm(1)
+    off_step(0)
     relay(3)
     mm(2)
+    off_step(1)
     mm(3)
     relay(4)
+    off_step(2)
     mm(4)
+    off_step(3)
+    off_end()
     relay(5)
     mm(5)
     relay(6)
@@ -222,6 +299,28 @@
         cp.start()
         tcopies.append(cp)
 
+    zs = (0, -1, 1, 2)
+    near = [(i, k, o) for i in offs for k in zs for o in (0, 1) if (i, k, o) != (0, 0, 0)]
+
+    def post(i, k, o):
+        return (offs.index(i) * 4 + zs.index(k)) * 2 + o
+
+    me = (x * 4 + zl) * 2 + c
+    ncopies = []
+    for n, (i, k, o) in enumerate(near):
+        to = chip(i, k)
+        core = 1 - c if o else c
+        to = to[:4] + (core,)
+        owner_at = (to[2] * 4 + to[3]) * 2 + core
+        slot = post(i if i == 2 else -i, k if k == 2 else -k, o)
+        for src, dst, ss, rr in ((packed.at[owner_at], rows_in.at[me], nsend, nrecv), (counts, counts_in.at[me], csend, crecv)):
+            cp = pltpu.make_async_remote_copy(
+                src_ref=src, dst_ref=dst, send_sem=ss.at[n], recv_sem=rr.at[slot], device_id=to, device_id_type=MESH)
+            cp.start()
+            ncopies.append(cp)
+    rows_in[me] = packed[me]
+    counts_in[me] = counts[...]
+
     T = M // 4
     H = part.shape[1] // 2
     left, right = pl.ds(0, H), pl.ds(H, H)
@@ -252,8 +351,6 @@
             src_ref=ysend.at[slot], dst_ref=yrecv.at[slot], send_sem=ysem.at[slot], recv_sem=yrsem.at[slot],
             device_id=partner, device_id_type=MESH).wait_recv()
 
-    bf = jnp.bfloat16
-    f32 = jnp.float32
     if ny > 1:
         partial(2)
         ysend[0] = part[quarter(2), left].astype(bf)
@@ -403,6 +500,37 @@
     qrelay(8)
     block(2, 2)
 
+    for i, k, o in near:
+        n = post(i, k, o)
+        for src, ref, ss, rr in ((packed, rows_in, nsend, nrecv), (None, counts_in, csend, crecv)):
+            pltpu.make_async_remote_copy(
+                src_ref=ref.at[0], dst_ref=ref.at[0], send_sem=ss.at[0], recv_sem=rr.at[n],
+                device_id=partner, device_id_type=MESH).wait_recv()
+    J = peers_in_pool * cap
+    width = counts.shape[1]
+    every = counts_in[...].reshape(peers_in_pool, width)
+    mine_only = jnp.where(lax.broadcasted_iota(i32, every.shape, 1) == me, every, 0.0)
+    count = jnp.sum(mine_only, axis=1, keepdims=True)
+    source = lax.broadcasted_iota(i32, (peers_in_pool, J), 0)
+    column_of = lax.broadcasted_iota(i32, (peers_in_pool, J), 1) // cap
+    valid = jnp.sum(jnp.where(source == column_of, count, 0.0), axis=0, keepdims=True)
+    ahead = jnp.sum(jnp.where(source < column_of, count, 0.0), axis=0, keepdims=True)
+    nth = lax.rem(lax.broadcasted_iota(i32, (1, J), 1), cap)
+    slot_of = lax.rem(head_ref[0] + ahead.astype(i32) + nth, B)
+    slot_of = jnp.where(nth < valid.astype(i32), slot_of, -1)
+    tile = min(256, B)
+
+    def write(r, carry):
+        first = pl.multiple_of(r * tile, tile)
+        spread = onehot(lax.broadcasted_iota(i32, (tile, J), 0) + first, slot_of)
+        fresh = jnp.dot(spread, rows_in[...].reshape(J, rows_in.shape[2]), preferred_element_type=f32)
+        hits = jnp.dot(spread, jnp.ones((J, rows_in.shape[2]), bf), preferred_element_type=f32)
+        old = bankbuf[pl.ds(pl.multiple_of(c * B + first, tile), tile), :]
+        newbank_ref[pl.ds(first, tile), :] = jnp.where(hits > 0.5, fresh, old.astype(f32)).astype(bf)
+        return carry
+
+    lax.fori_loop(0, B // tile, write, 0)
+
     stats[0] = sbuf[0]
     for i, k in far:
         pltpu.make_async_remote_copy(
@@ -423,24 +551,28 @@
     for k in range(2):
         out_ref[:, k * W:(k + 1) * W] = loss[k:k + 1, :]
 
-    for cp in sends + psends + swaps + tcopies + ycopies + qsends + scopies:
+    for cp in sends + psends + swaps + tcopies + ncopies + ycopies + qsends + scopies:
         cp.wait_send()
 
 
-def tower(tokens, w_hidden, w_out, bank, offsets, positives):
+def tower(tokens, w_hidden, w_out, bank, log_freq, item_ids, positives, new_items, new_owner, queue_head):
     M, K = tokens.shape[1:]
     R, N = w_hidden.shape
     E = w_out.shape[1]
     B = bank.shape[0]
     T = M // 4
+    L = item_ids.shape[1]
+    pool = K // R
+    cap = 2 * new_items.shape[0] // pool
     anywhere = pl.BlockSpec(memory_space=pl.ANY)
     vmem = pl.BlockSpec(memory_space=pltpu.VMEM)
     dma = pltpu.SemaphoreType.DMA
     return pl.pallas_call(
         tower_kernel,
-        out_shape=jax.ShapeDtypeStruct((1, T), jnp.float32),
-        in_specs=[anywhere, anywhere, vmem, anywhere, anywhere, vmem],
-        out_specs=vmem,
+        out_shape=(jax.ShapeDtypeStruct((1, T), jnp.float32), jax.ShapeDtypeStruct((B, E), jnp.bfloat16)),
+        in_specs=[anywhere, anywhere, vmem, anywhere, anywhere, vmem, vmem, vmem, vmem,
+                  pl.BlockSpec(memory_space=pltpu.SMEM)],
+        out_specs=(vmem, vmem),
         scratch_shapes=[
             pltpu.VMEM((16, M, 2 * R), jnp.bfloat16),
             pltpu.VMEM((2, K, N // 2), jnp.bfloat16),
@@ -449,93 +581,36 @@
             pltpu.VMEM((6, T, E // 2), jnp.bfloat16),
             pltpu.VMEM((6, T, E // 2), jnp.bfloat16),
             pltpu.VMEM((2 * B, E), jnp.bfloat16),
-            pltpu.VMEM((2 * B, offsets.shape[1]), jnp.float32),
+            pltpu.VMEM((2 * B, T // 2), jnp.float32),
             pltpu.VMEM((16, T, E), jnp.bfloat16),
             pltpu.VMEM((E, T), jnp.bfloat16),
             pltpu.VMEM((20, 1, T), jnp.int32),
             pltpu.VMEM((16, 8, T // 2), jnp.float32),
             pltpu.VMEM((20, 8, T // 2), jnp.float32),
+            pltpu.VMEM(log_freq.shape, jnp.bfloat16),
+            pltpu.VMEM((B, log_freq.shape[0] // 8), jnp.bfloat16),
+            pltpu.VMEM((B, L), jnp.int32),
+            pltpu.VMEM((B, L), jnp.float32),
+            pltpu.VMEM((pool, cap, E), jnp.bfloat16),
+            pltpu.VMEM((1, 128), jnp.float32),
+            pltpu.VMEM((pool, cap, E), jnp.bfloat16),
+            pltpu.VMEM((pool, 1, 128), jnp.float32),
             dma((16,)), dma((4,)), dma((40,)), dma((64,)), dma((64,)), dma((64,)),
             dma((2,)), dma((2,)), dma((6,)), dma((6,)), dma((40,)), dma((64,)),
-            dma((19,)), dma((20,)), dma((19,)), dma((20,)),
+            dma((19,)), dma((20,)), dma((19,)), dma((20,)), dma((31,)), dma((32,)), dma((31,)), dma((32,)),
         ],
         compiler_params=pltpu.CompilerParams(collective_id=0, has_side_effects=True, vmem_limit_bytes=56 * 1024 * 1024),
         name="tower",
-    )(tokens, w_hidden, w_out, bank, offsets, positives)
-
-
-def copy_for_each(x, axis):
-    copies = jnp.broadcast_to(x, (lax.axis_size(axis), *x.shape))
-    return lax.all_to_all(copies, axis, split_axis=0, concat_axis=0, tiled=True)
-
-
-def folded_in_pairs(pieces, combine):
-    while len(jax.tree.leaves(pieces)[0]) > 1:
-        pieces = jax.vmap(combine)(*(pieces[side::2] for side in (0, 1)))
-    return pieces[0]
-
-
-def entering(x, axis, combine, identity):
-    count, position = (lax.axis_size(axis), lax.axis_index(axis))
-    passed = jnp.arange(count) < position
-
-    def kept(part, zero, own):
-        part = jnp.where(
-            passed.reshape(-1, *(1 for _ in own.shape)), part, jnp.asarray(zero, own.dtype)
-        )
-        return part
-
-    pieces = copy_for_each(x, axis)
-    return folded_in_pairs(kept(pieces, identity, x), combine)
-
-
-def add_counts(earlier_part, later_part):
-    return earlier_part + later_part
+    )(tokens, w_hidden, w_out, bank, log_freq, item_ids, positives, new_items, new_owner, queue_head)
 
 
 def body(
     tokens, w_hidden, w_out, bank, item_ids, log_freq, positives, new_items, new_owner, queue_head
 ):
-    offsets = jnp.take(log_freq, item_ids).astype(jnp.float32) * LOG2E
-    offsets = jnp.broadcast_to(offsets[:, None], (bank.shape[0], 128))
-    query_loss = tower(tokens, w_hidden, w_out, bank, offsets, positives)
-    owners = new_owner[:, 0]
-    head_slot = queue_head[0]
-    shard_rows = bank.shape[0]
-    peer_count = lax.axis_size(POOL)
-    local_rows = new_items.shape[0]
-    capacity = 2 * local_rows // peer_count
-    onehot = (owners[:, None] == jnp.arange(peer_count, dtype=jnp.int32)[None, :]).astype(jnp.int32)
-    counts = jnp.sum(onehot, axis=0, dtype=jnp.int32)
-    before = jnp.sum(
-        (jnp.cumsum(onehot, axis=0, dtype=jnp.int32) - onehot) * onehot, axis=1, dtype=jnp.int32
+    return tower(
+        tokens, w_hidden, w_out, bank, log_freq.reshape(-1, 128), item_ids.reshape(-1, 128),
+        positives, new_items, new_owner.reshape(1, -1), queue_head,
     )
-    earlier = entering(counts, POOL, add_counts, jnp.zeros_like(counts))
-    ranks = before + jnp.sum(onehot * earlier[None, :], axis=1, dtype=jnp.int32)
-    send_pos = owners * capacity + before
-    rows_out = (
-        jnp.zeros((peer_count * capacity, new_items.shape[1]), jnp.bfloat16)
-        .at[send_pos]
-        .set(new_items)
-    )
-    ranks_out = jnp.full((peer_count * capacity,), -1, jnp.int32).at[send_pos].set(ranks)
-    rows_in, ranks_in = (
-        lax.all_to_all(
-            rows_out.reshape(peer_count, capacity, -1),
-            POOL,
-            split_axis=0,
-            concat_axis=0,
-            tiled=True,
-        ),
-        lax.all_to_all(
-            ranks_out.reshape(peer_count, capacity), POOL, split_axis=0, concat_axis=0, tiled=True
-        ),
-    )
-    local_slots = jnp.where(ranks_in >= 0, (head_slot + ranks_in) % shard_rows, shard_rows).reshape(
-        -1
-    )
-    new_bank = bank.at[local_slots].set(rows_in.reshape(-1, new_items.shape[1]), mode="drop")
-    return (query_loss, new_bank)
 
 
 def solution(mesh):

time: 142 us -> 100 us (0.70)
  starting transfers between devices: 21.8 us -> 0 us
  local copies, waits for them, and re-layouts: 18.9 us -> 3.07 us
  Pallas kernels: 89.6 us -> 94.8 us
  waiting for transfers between devices: 5.04 us -> 0 us
  other arithmetic: 4.49 us -> 0 us
    all_to_all x3 -> x0, starting transfers between devices: 21.8 us -> none  [the longest x1 9.05 us: copy_for_each(): return lax.all_to_all(copies, axis, split_axis=0, concat_axis=0, tiled=True)]
    gather x1 -> x0, local copies, waits for them, and re-layouts: 6.8 us -> none  [body(): offsets = jnp.take(log_freq, item_ids).astype(jnp.float32) * LOG2E]
    scatter x3 -> x0, local copies, waits for them, and re-layouts: 6.52 us -> none  [the longest x1 2.62 us: body(): bank.at[local_slots]]
    pallas_call x1, Pallas kernels: 89.6 us -> 94.8 us  [tower(): pl.pallas_call(tower_kernel, out_shape=(jax.ShapeDtypeStruct((1, T), jnp....]
    all_to_all x3 -> x0, waiting for transfers between devices: 5.04 us -> none  [the longest x1 5.04 us: copy_for_each(): return lax.all_to_all(copies, axis, split_axis=0, concat_axis=0, tiled=True)]
    broadcast_in_dim x2 -> x0, local copies, waits for them, and re-layouts: 1.6 us -> none  [the longest x1 0.99 us: body(): offsets = jnp.broadcast_to(offsets[:, None], (bank.shape[0], 128))]
    reduce_sum x2 -> x0, other arithmetic: 1.56 us -> none  [the longest x1 0.79 us: body(): counts = jnp.sum(onehot, axis=0, dtype=jnp.int32)]
    unnamed x12 -> x2, local copies, waits for them, and re-layouts: 2.83 us -> 3.07 us
  transfers between devices with their start and end apart: 3 -> 0, of which waited for: 1 -> 0; matrix products, arithmetic and copies ran while one was open for 9% -> 0% of each run, Pallas kernels for 63% -> 0%
where the time goes in v3:
time: 100 us; the launch traced here: 99.2 us
  Pallas kernels  94.8 us (95%)
  local copies, waits for them, and re-layouts  3.07 us (3%)
  between operations  1.29 us (1%)
    pallas_call x1, Pallas kernels, tower(): pl.pallas_call(tower_kernel, out_shape=(jax.ShapeDtypeStruct((1, T), jnp....  94.8 us
    unnamed x2, local copies, waits for them, and re-layouts  3.07 us

profile of v3, /device:TPU:2, one launch (start us, length us, event | category | flops | bytes accessed | tf_op | source)
XLA Modules:
  0.0 99.2 jit_solution(10848140406600019817)
XLA Ops:
  1.3 94.8 %tower.1 = (f32[1,256]{1,0:T(1,128)}, bf16[1024,256]{1,0:T(8,128)(2,1)}) custom-call(bf16[1,1024,4096]{2,1,0:T(8,128)(2,1)} %tok_hbm.1, bf16[128,1024]{1,0:T(8,128)(2,1)} %w_hbm.1, bf16[1024,256]{1,0:T(8,128)(2,1)} %wo_ref.1, bf16[1024,256]{1,0:T(8,128)(2,1)} %bank_hbm.1, bf16[8192,128]{1,0:T(8,128)(2,1)} %bitcast.3, s32[8,128]{1,0:T(8,128)} %bitcast.4, ...), custom_call_target="tpu_custom_call" | custom-call | tf_op jit(solution)/shard_map/tower/pallas_call | solution.py:570
  96.1 1.2 %copy.15 = f32[1,256]{1,0:T(1,128)} copy(f32[1,256]{1,0:T(1,128)} %get-tuple-element.4) | data formatting | bytes 2048
  97.3 1.9 %copy.16 = bf16[1024,256]{1,0:T(8,128)(2,1)} copy(bf16[1024,256]{1,0:T(8,128)(2,1)} %get-tuple-element.5) | data formatting | bytes 1048576

commit v4 on v3

--- a/solution.py
+++ b/solution.py
@@ -16,13 +16,14 @@
 
 LOG2E = 1.4426950408889634
 LN2 = 0.6931471805599453
+SCALE = 5.0 * LOG2E
 
 
 def tower_kernel(tok_hbm, w_hbm, wo_ref, bank_hbm, freq_hbm, ids_ref, pos_ref, items_ref,
                  owner_ref, head_ref, out_ref, newbank_ref, tok, wbuf, acc, part, ysend, yrecv,
                  bankbuf, offb, qbuf, qt, tbuf, sbuf, stats, table, pick, where_at, found, packed, counts, rows_in, counts_in, tok_sem, own_sem, send_sem, recv_sem, psend, precv,
                  xsend, xrecv, ysem, yrsem, qsend, qrecv, tsend, trecv, ssend, srecv,
-                 nsend, nrecv, csend, crecv):
+                 nsend, nrecv, csend, crecv, osend, orecv):
     dp, y, x, zl, c = (lax.axis_index(a) for a in AXES)
     ny = lax.axis_size("tensor")
     pz = dp * 4 + zl
@@ -42,6 +43,16 @@
 
     partner = (dp, y, x, zl, 1 - c)
 
+    def arrived(ref, sem):
+        pltpu.make_async_remote_copy(
+            src_ref=ref, dst_ref=ref, send_sem=send_sem.at[0], recv_sem=sem,
+            device_id=partner, device_id_type=MESH).wait_recv()
+
+    def sent(ref, sem):
+        pltpu.make_async_remote_copy(
+            src_ref=ref, dst_ref=ref, send_sem=sem, recv_sem=recv_sem.at[0],
+            device_id=partner, device_id_type=MESH).wait_send()
+
     def column(step):
         return (dp, lax.rem(y + step + ny, ny), x, zl, c)
 
@@ -64,7 +75,7 @@
         nf, ns = kind
         ref = view(h, f, s, piece, c)
         cp = pltpu.make_async_remote_copy(
-            src_ref=ref, dst_ref=ref, send_sem=send_sem.at[len(sends)],
+            src_ref=ref, dst_ref=ref, send_sem=send_sem.at[0],
             recv_sem=recv_sem.at[key(h, nf, ns, piece)],
             device_id=along(h, first, step), device_id_type=MESH)
         cp.start()
@@ -75,7 +86,7 @@
     def to_partner(h, f, s, piece):
         ref = view(h, f, s, piece, c)
         cp = pltpu.make_async_remote_copy(
-            src_ref=ref, dst_ref=ref, send_sem=psend.at[key(h, f, s, piece)],
+            src_ref=ref, dst_ref=ref, send_sem=psend.at[0],
             recv_sem=precv.at[key(h, f, s, piece)], device_id=partner, device_id_type=MESH)
         cp.start()
         psends.append(cp)
@@ -106,12 +117,12 @@
     barrier = pltpu.get_barrier_semaphore()
     peers = [chip(1, 0), chip(-1, 0), chip(0, 1), chip(0, -1), partner]
     if ny > 1:
-        peers += [column(1), column(-1)]
+        peers += [column(step) for step in range(1, ny)]
     for p in peers:
         pl.semaphore_signal(barrier, inc=1, device_id=p, device_id_type=MESH)
 
     groups = [[(0, 0)], [(-1, 0), (1, 0)], [(0, -1), (0, 1)], [(2, 0)],
-              [(-1, -1), (-1, 1), (1, -1), (1, 1)], [(0, 2)], [(2, -1), (2, 1)], [(-1, 2), (1, 2)], [(2, 2)]]
+              [(-1, -1), (-1, 1)], [(1, -1), (1, 1)], [(0, 2)], [(2, -1), (2, 1)], [(-1, 2), (1, 2)], [(2, 2)]]
 
     tok_wait = {}
     n = 0
@@ -133,10 +144,10 @@
     pl.semaphore_wait(barrier, len(peers))
 
     for h in (0, 1):
+        to_partner(h, 0, 0, None)
+    for h in (0, 1):
         for step in (1, -1):
             send(h, 0, 0, None, True, step, (-step, 0))
-    for h in (0, 1):
-        to_partner(h, 0, 0, None)
     for h in (0, 1):
         for step in (1, -1):
             send(h, 0, 0, None, False, step, (0, -step))
@@ -183,9 +194,13 @@
     L = ids_ref.shape[1]
     A = table.shape[0] // 8
 
+    G = ids_ref.shape[0] // ny
+    OR = B // ny
+    here_rows = pl.ds(pl.multiple_of(c * B + y * OR, OR), OR)
+
     def off_start():
-        for g in range(ids_ref.shape[0]):
-            row = ids_ref[g:g + 1, :].astype(f32)
+        for g in range(G):
+            row = ids_ref[pl.ds(y * G + g, 1), :].astype(f32)
             idx = jnp.transpose(jnp.broadcast_to(row, (L, L))).astype(i32)
             where_at[pl.ds(g * L, L), :] = idx
             line = lax.rem(idx // L, A)
@@ -195,7 +210,7 @@
     def off_step(j):
         if j == 0:
             freq_copy.wait()
-        tile = min(256, B)
+        tile = min(256, OR)
 
         def rows_step(r, carry):
             rs = pl.ds(pl.multiple_of(r * tile, tile), tile)
@@ -209,12 +224,20 @@
                 found[rs, :] = found[rs, :] + got
             return carry
 
-        lax.fori_loop(0, B // tile, rows_step, 0)
+        lax.fori_loop(0, OR // tile, rows_step, 0)
 
     def off_end():
-        lane_at = lax.broadcasted_iota(i32, (B, L), 1)
+        lane_at = lax.broadcasted_iota(i32, (OR, L), 1)
         val = jnp.sum(jnp.where(lax.rem(where_at[...], L) == lane_at, found[...], 0.0), axis=1, keepdims=True)
-        offb[mine, :] = jnp.broadcast_to(val * LOG2E, (B, offb.shape[1]))
+        offb[here_rows, :] = jnp.broadcast_to(val * LOG2E, (OR, offb.shape[1]))
+        for step in range(1, ny):
+            pltpu.make_async_remote_copy(
+                src_ref=offb.at[here_rows, :], dst_ref=offb.at[here_rows, :], send_sem=osend.at[0],
+                recv_sem=orecv.at[0], device_id=column(step), device_id_type=MESH).start()
+
+    def off_collect():
+        if ny > 1:
+            arrived(offb.at[pl.ds(0, (ny - 1) * OR), :], orecv.at[0])
         swap(offb)
 
     def relay(g):
@@ -222,6 +245,8 @@
             for h in (0, 1):
                 for p in pieces(f, s):
                     wait_link(h, f, s, p)
+                for p in pieces(f, s):
+                    to_partner(h, f, s, p)
                 if s == 0 and f != 2:
                     send(h, f, 0, 0 if f == -1 else 1, True, -f, (2, 0))
                 if s == 0:
@@ -229,8 +254,6 @@
                         send(h, f, 0, None, False, step, (f, -step))
                 elif s != 2:
                     send(h, f, s, 0 if s == -1 else 1, False, -s, (f, 2))
-                for p in pieces(f, s):
-                    to_partner(h, f, s, p)
 
     def mm(g):
         items = groups[g]
@@ -260,28 +283,31 @@
 
     pack()
     mm(0)
+    off_start()
     relay(1)
-    off_start()
+    off_step(0)
+    off_step(1)
     relay(2)
     mm(1)
-    off_step(0)
+    off_step(2)
+    off_step(3)
+    off_end()
     relay(3)
     mm(2)
-    off_step(1)
+    relay(4)
     mm(3)
-    relay(4)
-    off_step(2)
+    relay(5)
     mm(4)
-    off_step(3)
-    off_end()
-    relay(5)
+    relay(6)
     mm(5)
-    relay(6)
+    relay(7)
     mm(6)
-    relay(7)
+    off_collect()
+    relay(8)
     mm(7)
-    relay(8)
+    relay(9)
     mm(8)
+    mm(9)
 
     far = [(i, k) for i in offs for k in (0, -1, 1, 2, -2) if (i, k) != (0, 0)]
 
@@ -294,16 +320,13 @@
     tcopies = []
     for n, (i, k) in enumerate(far):
         cp = pltpu.make_async_remote_copy(
-            src_ref=pos_ref, dst_ref=tbuf.at[mirror(i, k)], send_sem=tsend.at[n], recv_sem=trecv.at[mirror(i, k)],
+            src_ref=pos_ref, dst_ref=tbuf.at[mirror(i, k)], send_sem=tsend.at[0], recv_sem=trecv.at[0],
             device_id=chip(i, k), device_id_type=MESH)
         cp.start()
         tcopies.append(cp)
 
     zs = (0, -1, 1, 2)
     near = [(i, k, o) for i in offs for k in zs for o in (0, 1) if (i, k, o) != (0, 0, 0)]
-
-    def post(i, k, o):
-        return (offs.index(i) * 4 + zs.index(k)) * 2 + o
 
     me = (x * 4 + zl) * 2 + c
     ncopies = []
@@ -312,10 +335,9 @@
         core = 1 - c if o else c
         to = to[:4] + (core,)
         owner_at = (to[2] * 4 + to[3]) * 2 + core
-        slot = post(i if i == 2 else -i, k if k == 2 else -k, o)
         for src, dst, ss, rr in ((packed.at[owner_at], rows_in.at[me], nsend, nrecv), (counts, counts_in.at[me], csend, crecv)):
             cp = pltpu.make_async_remote_copy(
-                src_ref=src, dst_ref=dst, send_sem=ss.at[n], recv_sem=rr.at[slot], device_id=to, device_id_type=MESH)
+                src_ref=src, dst_ref=dst, send_sem=ss.at[0], recv_sem=rr.at[0], device_id=to, device_id_type=MESH)
             cp.start()
             ncopies.append(cp)
     rows_in[me] = packed[me]
@@ -341,14 +363,14 @@
 
     def ysend_to(slot, step):
         cp = pltpu.make_async_remote_copy(
-            src_ref=ysend.at[slot], dst_ref=yrecv.at[slot], send_sem=ysem.at[slot], recv_sem=yrsem.at[slot],
+            src_ref=ysend.at[slot], dst_ref=yrecv.at[slot], send_sem=ysem.at[0], recv_sem=yrsem.at[slot],
             device_id=column(step), device_id_type=MESH)
         cp.start()
         ycopies.append(cp)
 
     def ywait(slot):
         pltpu.make_async_remote_copy(
-            src_ref=ysend.at[slot], dst_ref=yrecv.at[slot], send_sem=ysem.at[slot], recv_sem=yrsem.at[slot],
+            src_ref=ysend.at[slot], dst_ref=yrecv.at[slot], send_sem=ysem.at[0], recv_sem=yrsem.at[slot],
             device_id=partner, device_id_type=MESH).wait_recv()
 
     if ny > 1:
@@ -375,11 +397,11 @@
         ywait(4)
         ywait(5)
         own_q = quarter(0)
-        qbuf[0, :, left] = (part[own_q, left] + yrecv[3].astype(f32) + yrecv[4].astype(f32)).astype(bf)
-        qbuf[0, :, right] = (part[own_q, right] + yrecv[2].astype(f32) + yrecv[5].astype(f32)).astype(bf)
+        qbuf[0, :, left] = ((part[own_q, left] + yrecv[3].astype(f32) + yrecv[4].astype(f32)) * SCALE).astype(bf)
+        qbuf[0, :, right] = ((part[own_q, right] + yrecv[2].astype(f32) + yrecv[5].astype(f32)) * SCALE).astype(bf)
     else:
         partial(0)
-        qbuf[0] = part[pl.ds(0, T), :].astype(bf)
+        qbuf[0] = (part[pl.ds(0, T), :] * SCALE).astype(bf)
 
     P2 = T // 2
     P4 = T // 4
@@ -393,7 +415,7 @@
 
     def qgo(h, f, s, piece, first, step, kind):
         cp = pltpu.make_async_remote_copy(
-            src_ref=qview(h, f, s, piece), dst_ref=qview(h, kind[0], kind[1], piece), send_sem=qsend.at[len(qsends)],
+            src_ref=qview(h, f, s, piece), dst_ref=qview(h, kind[0], kind[1], piece), send_sem=qsend.at[0],
             recv_sem=qrecv.at[key(h, kind[0], kind[1], piece)],
             device_id=along(h, first, step), device_id_type=MESH)
         cp.start()
@@ -426,10 +448,7 @@
     for cp in swaps:
         cp.wait_recv()
     tbuf[0] = pos_ref[...]
-    for i, k in far:
-        pltpu.make_async_remote_copy(
-            src_ref=pos_ref, dst_ref=tbuf.at[spot(i, k)], send_sem=tsend.at[0], recv_sem=trecv.at[spot(i, k)],
-            device_id=partner, device_id_type=MESH).wait_recv()
+    arrived(tbuf.at[pl.ds(1, len(far))], trecv.at[0])
 
     base = (x * 4 + zl) * (2 * B)
     CH = min(512, 2 * B)
@@ -437,75 +456,87 @@
     lower = lax.rem(lane, P2) < P4
     sub = lax.broadcasted_iota(jnp.int32, (8, T), 0)
     W = sbuf.shape[2]
-    scopies = []
-
-    def block(dx, dz):
-        slot = offs.index(dx) * 4 + offs.index(dz)
-        qt[...] = jnp.transpose(qbuf[slot])
-        if dz == 2:
-            target = jnp.where(lower, tbuf[spot(dx, -2)], tbuf[spot(dx, 2)])
+
+    SUB = min(64, CH)
+    G8 = SUB // 8
+    levels = G8.bit_length() - 1
+
+    def pick_of(values, i):
+        return sum(jnp.where(i == k, v, 0) for k, v in enumerate(values))
+
+    def blocks(items):
+        def one(i, carry):
+            dx = pick_of([a for a, _ in items], i)
+            dz = pick_of([b for _, b in items], i)
+            ix = jnp.where(dx == -1, 1, jnp.where(dx == 1, 2, jnp.where(dx == 2, 3, 0)))
+            iz = jnp.where(dz == -1, 1, jnp.where(dz == 1, 2, jnp.where(dz == 2, 3, 0)))
+            slot = ix * 4 + iz
+            qt[...] = jnp.transpose(qbuf[slot])
+            target = tbuf[ix * 5 + iz]
+            target = jnp.where(jnp.logical_and(lower, jnp.broadcast_to(iz, lower.shape) == 3), tbuf[ix * 5 + 4], target)
+            t = jnp.broadcast_to(target - base, (8, T))
+            group = lax.shift_right_arithmetic(t, 3)
+            bits = [jnp.bitwise_and(lax.shift_right_arithmetic(group, b), 1) == 1 for b in range(levels)]
+            which = lax.shift_right_arithmetic(group, levels)
+            m = total = None
+            hit = jnp.zeros((8, T), f32)
+            for k in range(2 * B // CH):
+                rows = pl.ds(k * CH, CH)
+                prod = jnp.dot(bankbuf[rows, :], qt[...], preferred_element_type=f32)
+                off = offb[rows, :]
+                if T > off.shape[1]:
+                    off = jnp.concatenate([off] * (T // off.shape[1]), axis=1)
+                every_logit = (prod - off).reshape(CH // SUB, G8, 8, T)
+                for u in range(CH // SUB):
+                    logit = every_logit[u]
+                    high = jnp.max(logit, axis=0)
+                    top = high if m is None else jnp.maximum(m, high)
+                    chosen = [logit[r] for r in range(G8)]
+                    for b in range(levels):
+                        chosen = [jnp.where(bits[b], chosen[2 * r + 1], chosen[2 * r]) for r in range(len(chosen) // 2)]
+                    hit = jnp.where(which == k * (CH // SUB) + u, chosen[0], hit)
+                    gain = jnp.sum(jnp.exp2(logit - top[None]), axis=0)
+                    total = gain if m is None else total * jnp.exp2(m - top) + gain
+                    m = top
+            top = jnp.max(m, axis=0, keepdims=True)
+            total = jnp.sum(total * jnp.exp2(m - top), axis=0, keepdims=True)
+            score = jnp.sum(jnp.where(jnp.bitwise_and(t, 7) == sub, hit, 0.0), axis=0, keepdims=True)
+            for n, v in enumerate((top, total, score)):
+                for k in range(2):
+                    sbuf[slot, pl.ds(n * 2 + k, 1), :] = v[:, k * W:(k + 1) * W]
+            return carry
+
+        if len(items) == 1:
+            one(0, 0)
         else:
-            target = tbuf[spot(dx, dz)]
-        t = jnp.broadcast_to(target - base, (8, T))
-        group = lax.shift_right_arithmetic(t, 3)
-
-        def chunk(k, carry):
-            m, total, hit = carry
-            rows = pl.ds(pl.multiple_of(k * CH, CH), CH)
-            prod = jnp.dot(bankbuf[rows, :], qt[...], preferred_element_type=f32)
-            off = offb[rows, :]
-            if T > off.shape[1]:
-                off = jnp.concatenate([off] * (T // off.shape[1]), axis=1)
-            logit = (prod * (5.0 * LOG2E) - off).reshape(CH // 8, 8, T)
-            top = jnp.maximum(m, jnp.max(logit, axis=0))
-            here = group - k * (CH // 8)
-            for r in range(CH // 8):
-                hit = jnp.where(here == r, logit[r], hit)
-            total = total * jnp.exp2(m - top) + jnp.sum(jnp.exp2(logit - top[None]), axis=0)
-            return top, total, hit
-
-        zero = jnp.zeros((8, T), f32)
-        m, total, hit = lax.fori_loop(0, 2 * B // CH, chunk, (jnp.full((8, T), -jnp.inf, f32), zero, zero))
-        top = jnp.max(m, axis=0, keepdims=True)
-        total = jnp.sum(total * jnp.exp2(m - top), axis=0, keepdims=True)
-        score = jnp.sum(jnp.where(jnp.bitwise_and(t, 7) == sub, hit, 0.0), axis=0, keepdims=True)
-        for n, v in enumerate((top, total, score)):
-            for k in range(2):
-                sbuf[slot, pl.ds(n * 2 + k, 1), :] = v[:, k * W:(k + 1) * W]
-        for k in ((dz,) if dz != 2 else (2, -2)):
-            if (dx, k) == (0, 0):
-                continue
-            cp = pltpu.make_async_remote_copy(
-                src_ref=sbuf.at[slot], dst_ref=stats.at[mirror(dx, k)], send_sem=ssend.at[len(scopies)],
-                recv_sem=srecv.at[mirror(dx, k)], device_id=chip(dx, k), device_id_type=MESH)
-            cp.start()
-            scopies.append(cp)
-
-    block(0, 0)
+            lax.fori_loop(0, len(items), one, 0)
+        for dx, dz in items:
+            for k in ((dz,) if dz != 2 else (2, -2)):
+                if (dx, k) == (0, 0):
+                    continue
+                cp = pltpu.make_async_remote_copy(
+                    src_ref=sbuf.at[offs.index(dx) * 4 + offs.index(dz)], dst_ref=stats.at[mirror(dx, k)],
+                    send_sem=ssend.at[0], recv_sem=srecv.at[0], device_id=chip(dx, k), device_id_type=MESH)
+                cp.start()
+
+    blocks([(0, 0)])
     qrelay(1)
     qrelay(2)
-    for dx, dz in ((-1, 0), (1, 0), (0, -1), (0, 1)):
-        block(dx, dz)
+    blocks([(-1, 0), (1, 0), (0, -1), (0, 1)])
     qrelay(3)
     qrelay(4)
-    for dx, dz in ((-1, -1), (-1, 1), (1, -1), (1, 1)):
-        block(dx, dz)
     qrelay(5)
-    block(2, 0)
-    block(0, 2)
+    blocks([(-1, -1), (-1, 1), (1, -1), (1, 1)])
     qrelay(6)
+    blocks([(2, 0), (0, 2)])
     qrelay(7)
-    for dx, dz in ((2, -1), (2, 1), (-1, 2), (1, 2)):
-        block(dx, dz)
     qrelay(8)
-    block(2, 2)
-
-    for i, k, o in near:
-        n = post(i, k, o)
-        for src, ref, ss, rr in ((packed, rows_in, nsend, nrecv), (None, counts_in, csend, crecv)):
-            pltpu.make_async_remote_copy(
-                src_ref=ref.at[0], dst_ref=ref.at[0], send_sem=ss.at[0], recv_sem=rr.at[n],
-                device_id=partner, device_id_type=MESH).wait_recv()
+    blocks([(2, -1), (2, 1), (-1, 2), (1, 2)])
+    qrelay(9)
+    blocks([(2, 2)])
+
+    arrived(rows_in.at[pl.ds(0, len(near))], nrecv.at[0])
+    arrived(counts_in.at[pl.ds(0, len(near))], crecv.at[0])
     J = peers_in_pool * cap
     width = counts.shape[1]
     every = counts_in[...].reshape(peers_in_pool, width)
@@ -532,10 +563,7 @@
     lax.fori_loop(0, B // tile, write, 0)
 
     stats[0] = sbuf[0]
-    for i, k in far:
-        pltpu.make_async_remote_copy(
-            src_ref=sbuf.at[0], dst_ref=stats.at[spot(i, k)], send_sem=ssend.at[0], recv_sem=srecv.at[spot(i, k)],
-            device_id=partner, device_id_type=MESH).wait_recv()
+    arrived(stats.at[pl.ds(1, len(far))], srecv.at[0])
     low = lax.broadcasted_iota(jnp.int32, (8, W), 1) < P4
     parts = []
     for i in offs:
@@ -551,8 +579,18 @@
     for k in range(2):
         out_ref[:, k * W:(k + 1) * W] = loss[k:k + 1, :]
 
-    for cp in sends + psends + swaps + tcopies + ncopies + ycopies + qsends + scopies:
+    sent(wbuf.at[0, pl.ds(0, 30 * R), :], send_sem.at[0])
+    sent(wbuf.at[0], psend.at[0])
+    sent(tbuf.at[pl.ds(1, len(far))], tsend.at[0])
+    sent(rows_in.at[pl.ds(0, len(near))], nsend.at[0])
+    sent(counts_in.at[pl.ds(0, len(near))], csend.at[0])
+    sent(qbuf.at[pl.ds(0, 15)], qsend.at[0])
+    sent(stats.at[pl.ds(1, len(far))], ssend.at[0])
+    for cp in swaps:
         cp.wait_send()
+    if ny > 1:
+        sent(ysend, ysem.at[0])
+        sent(offb.at[pl.ds(0, (ny - 1) * OR), :], osend.at[0])
 
 
 def tower(tokens, w_hidden, w_out, bank, log_freq, item_ids, positives, new_items, new_owner, queue_head):
@@ -563,6 +601,7 @@
     T = M // 4
     L = item_ids.shape[1]
     pool = K // R
+    OR = B // lax.axis_size("tensor")
     cap = 2 * new_items.shape[0] // pool
     anywhere = pl.BlockSpec(memory_space=pl.ANY)
     vmem = pl.BlockSpec(memory_space=pltpu.VMEM)
@@ -588,16 +627,17 @@
             pltpu.VMEM((16, 8, T // 2), jnp.float32),
             pltpu.VMEM((20, 8, T // 2), jnp.float32),
             pltpu.VMEM(log_freq.shape, jnp.bfloat16),
-            pltpu.VMEM((B, log_freq.shape[0] // 8), jnp.bfloat16),
-            pltpu.VMEM((B, L), jnp.int32),
-            pltpu.VMEM((B, L), jnp.float32),
+            pltpu.VMEM((OR, log_freq.shape[0] // 8), jnp.bfloat16),
+            pltpu.VMEM((OR, L), jnp.int32),
+            pltpu.VMEM((OR, L), jnp.float32),
             pltpu.VMEM((pool, cap, E), jnp.bfloat16),
             pltpu.VMEM((1, 128), jnp.float32),
             pltpu.VMEM((pool, cap, E), jnp.bfloat16),
             pltpu.VMEM((pool, 1, 128), jnp.float32),
-            dma((16,)), dma((4,)), dma((40,)), dma((64,)), dma((64,)), dma((64,)),
-            dma((2,)), dma((2,)), dma((6,)), dma((6,)), dma((40,)), dma((64,)),
-            dma((19,)), dma((20,)), dma((19,)), dma((20,)), dma((31,)), dma((32,)), dma((31,)), dma((32,)),
+            dma((16,)), dma((4,)), dma((1,)), dma((64,)), dma((1,)), dma((64,)),
+            dma((2,)), dma((2,)), dma((1,)), dma((6,)), dma((1,)), dma((64,)),
+            dma((1,)), dma((1,)), dma((1,)), dma((1,)), dma((1,)), dma((1,)), dma((1,)), dma((1,)),
+            dma((1,)), dma((1,)),
         ],
         compiler_params=pltpu.CompilerParams(collective_id=0, has_side_effects=True, vmem_limit_bytes=56 * 1024 * 1024),
         name="tower",

time: 100 us -> 78.9 us (0.79)
  Pallas kernels: 94.8 us -> 74.3 us
    pallas_call x1, Pallas kernels: 94.8 us -> 74.3 us  [tower(): pl.pallas_call(tower_kernel, out_shape=(jax.ShapeDtypeStruct((1, T), jnp....]
where the time goes in v4:
time: 78.9 us; the launch traced here: 78.7 us
  Pallas kernels  74.3 us (94%)
  local copies, waits for them, and re-layouts  3.07 us (4%)
  between operations  1.29 us (2%)
    pallas_call x1, Pallas kernels, tower(): pl.pallas_call(tower_kernel, out_shape=(jax.ShapeDtypeStruct((1, T), jnp....  74.3 us
    unnamed x2, local copies, waits for them, and re-layouts  3.07 us

profile of v4, /device:TPU:2, one launch (start us, length us, event | category | flops | bytes accessed | tf_op | source)
XLA Modules:
  0.0 78.7 jit_solution(4755914696121964954)
XLA Ops:
  1.3 74.3 %tower.1 = (f32[1,256]{1,0:T(1,128)}, bf16[1024,256]{1,0:T(8,128)(2,1)}) custom-call(bf16[1,1024,4096]{2,1,0:T(8,128)(2,1)} %tok_hbm.1, bf16[128,1024]{1,0:T(8,128)(2,1)} %w_hbm.1, bf16[1024,256]{1,0:T(8,128)(2,1)} %wo_ref.1, bf16[1024,256]{1,0:T(8,128)(2,1)} %bank_hbm.1, bf16[8192,128]{1,0:T(8,128)(2,1)} %bitcast.3, s32[8,128]{1,0:T(8,128)} %bitcast.4, ...), custom_call_target="tpu_custom_call" | custom-call | tf_op jit(solution)/shard_map/tower/pallas_call | solution.py:609
  75.6 1.2 %copy.15 = f32[1,256]{1,0:T(1,128)} copy(f32[1,256]{1,0:T(1,128)} %get-tuple-element.4) | data formatting | bytes 2048
  76.8 1.9 %copy.16 = bf16[1024,256]{1,0:T(8,128)(2,1)} copy(bf16[1024,256]{1,0:T(8,128)(2,1)} %get-tuple-element.5) | data formatting | bytes 1048576

commit v5 on v4

--- a/solution.py
+++ b/solution.py
@@ -21,7 +21,7 @@
 
 def tower_kernel(tok_hbm, w_hbm, wo_ref, bank_hbm, freq_hbm, ids_ref, pos_ref, items_ref,
                  owner_ref, head_ref, out_ref, newbank_ref, tok, wbuf, acc, part, ysend, yrecv,
-                 bankbuf, offb, qbuf, qt, tbuf, sbuf, stats, table, pick, where_at, found, packed, counts, rows_in, counts_in, tok_sem, own_sem, send_sem, recv_sem, psend, precv,
+                 bankbuf, offb, qbuf, qt0, qt1, logits0, logits1, tbuf, sbuf, stats, table, pick, where_at, found, packed, counts, rows_in, counts_in, tok_sem, own_sem, send_sem, recv_sem, psend, precv,
                  xsend, xrecv, ysem, yrsem, qsend, qrecv, tsend, trecv, ssend, srecv,
                  nsend, nrecv, csend, crecv, osend, orecv):
     dp, y, x, zl, c = (lax.axis_index(a) for a in AXES)
@@ -317,31 +317,32 @@
     def mirror(i, k):
         return spot(i if i == 2 else -i, -k)
 
-    tcopies = []
-    for n, (i, k) in enumerate(far):
-        cp = pltpu.make_async_remote_copy(
-            src_ref=pos_ref, dst_ref=tbuf.at[mirror(i, k)], send_sem=tsend.at[0], recv_sem=trecv.at[0],
-            device_id=chip(i, k), device_id_type=MESH)
-        cp.start()
-        tcopies.append(cp)
-
     zs = (0, -1, 1, 2)
     near = [(i, k, o) for i in offs for k in zs for o in (0, 1) if (i, k, o) != (0, 0, 0)]
 
     me = (x * 4 + zl) * 2 + c
-    ncopies = []
-    for n, (i, k, o) in enumerate(near):
-        to = chip(i, k)
-        core = 1 - c if o else c
-        to = to[:4] + (core,)
-        owner_at = (to[2] * 4 + to[3]) * 2 + core
-        for src, dst, ss, rr in ((packed.at[owner_at], rows_in.at[me], nsend, nrecv), (counts, counts_in.at[me], csend, crecv)):
-            cp = pltpu.make_async_remote_copy(
-                src_ref=src, dst_ref=dst, send_sem=ss.at[0], recv_sem=rr.at[0], device_id=to, device_id_type=MESH)
-            cp.start()
-            ncopies.append(cp)
     rows_in[me] = packed[me]
     counts_in[me] = counts[...]
+
+    def post():
+        tcopies = []
+        for n, (i, k) in enumerate(far):
+            cp = pltpu.make_async_remote_copy(
+                src_ref=pos_ref, dst_ref=tbuf.at[mirror(i, k)], send_sem=tsend.at[0], recv_sem=trecv.at[0],
+                device_id=chip(i, k), device_id_type=MESH)
+            cp.start()
+            tcopies.append(cp)
+        ncopies = []
+        for n, (i, k, o) in enumerate(near):
+            to = chip(i, k)
+            core = 1 - c if o else c
+            to = to[:4] + (core,)
+            owner_at = (to[2] * 4 + to[3]) * 2 + core
+            for src, dst, ss, rr in ((packed.at[owner_at], rows_in.at[me], nsend, nrecv), (counts, counts_in.at[me], csend, crecv)):
+                cp = pltpu.make_async_remote_copy(
+                    src_ref=src, dst_ref=dst, send_sem=ss.at[0], recv_sem=rr.at[0], device_id=to, device_id_type=MESH)
+                cp.start()
+                ncopies.append(cp)
 
     T = M // 4
     H = part.shape[1] // 2
@@ -385,6 +386,7 @@
         partial(1)
         ysend[3] = part[quarter(1), left].astype(bf)
         ysend_to(3, 1)
+        post()
         ywait(0)
         ysend[4] = (yrecv[0].astype(f32) + part[quarter(-1), left]).astype(bf)
         ysend_to(4, -1)
@@ -400,6 +402,7 @@
         qbuf[0, :, left] = ((part[own_q, left] + yrecv[3].astype(f32) + yrecv[4].astype(f32)) * SCALE).astype(bf)
         qbuf[0, :, right] = ((part[own_q, right] + yrecv[2].astype(f32) + yrecv[5].astype(f32)) * SCALE).astype(bf)
     else:
+        post()
         partial(0)
         qbuf[0] = (part[pl.ds(0, T), :] * SCALE).astype(bf)
 
@@ -451,7 +454,7 @@
     arrived(tbuf.at[pl.ds(1, len(far))], trecv.at[0])
 
     base = (x * 4 + zl) * (2 * B)
-    CH = min(512, 2 * B)
+    CH = min(1024, 2 * B)
     lane = lax.broadcasted_iota(jnp.int32, (1, T), 1)
     lower = lax.rem(lane, P2) < P4
     sub = lax.broadcasted_iota(jnp.int32, (8, T), 0)
@@ -464,52 +467,65 @@
     def pick_of(values, i):
         return sum(jnp.where(i == k, v, 0) for k, v in enumerate(values))
 
-    def blocks(items):
-        def one(i, carry):
-            dx = pick_of([a for a, _ in items], i)
-            dz = pick_of([b for _, b in items], i)
-            ix = jnp.where(dx == -1, 1, jnp.where(dx == 1, 2, jnp.where(dx == 2, 3, 0)))
-            iz = jnp.where(dz == -1, 1, jnp.where(dz == 1, 2, jnp.where(dz == 2, 3, 0)))
+    def place(items, i):
+        if isinstance(i, int):
+            return tuple(offs.index(v) for v in items[i])
+        return tuple(pick_of([offs.index(item[d]) for item in items], i) for d in (0, 1))
+
+    def turn(at, qt):
+        qt[...] = jnp.transpose(qbuf[at[0] * 4 + at[1]])
+
+    def multiply(rows, logits, qt):
+        prod = jnp.dot(bankbuf[rows, :], qt[...], preferred_element_type=f32)
+        off = offb[rows, :]
+        if T > off.shape[1]:
+            off = jnp.concatenate([off] * (T // off.shape[1]), axis=1)
+        logits[rows, :] = prod - off
+
+    def block(ahead, logits_ahead, qt, at, logits):
+        if ahead is not None:
+            turn(ahead, qt)
+        if at is not None:
+            ix, iz = at
             slot = ix * 4 + iz
-            qt[...] = jnp.transpose(qbuf[slot])
             target = tbuf[ix * 5 + iz]
-            target = jnp.where(jnp.logical_and(lower, jnp.broadcast_to(iz, lower.shape) == 3), tbuf[ix * 5 + 4], target)
+            behind = jnp.logical_and(lower, jnp.broadcast_to(iz, lower.shape) == 3)
+            target = jnp.where(behind, tbuf[ix * 5 + 4], target)
             t = jnp.broadcast_to(target - base, (8, T))
             group = lax.shift_right_arithmetic(t, 3)
+            which = lax.shift_right_arithmetic(group, levels)
+
+        def chunk(k, carry):
+            first = pl.multiple_of(k * CH, CH)
+            if ahead is not None:
+                multiply(pl.ds(first, CH), logits_ahead, qt)
+            if at is None:
+                return carry
+            m, total, hit = carry
             bits = [jnp.bitwise_and(lax.shift_right_arithmetic(group, b), 1) == 1 for b in range(levels)]
-            which = lax.shift_right_arithmetic(group, levels)
-            m = total = None
-            hit = jnp.zeros((8, T), f32)
-            for k in range(2 * B // CH):
-                rows = pl.ds(k * CH, CH)
-                prod = jnp.dot(bankbuf[rows, :], qt[...], preferred_element_type=f32)
-                off = offb[rows, :]
-                if T > off.shape[1]:
-                    off = jnp.concatenate([off] * (T // off.shape[1]), axis=1)
-                every_logit = (prod - off).reshape(CH // SUB, G8, 8, T)
-                for u in range(CH // SUB):
-                    logit = every_logit[u]
-                    high = jnp.max(logit, axis=0)
-                    top = high if m is None else jnp.maximum(m, high)
-                    chosen = [logit[r] for r in range(G8)]
-                    for b in range(levels):
-                        chosen = [jnp.where(bits[b], chosen[2 * r + 1], chosen[2 * r]) for r in range(len(chosen) // 2)]
-                    hit = jnp.where(which == k * (CH // SUB) + u, chosen[0], hit)
-                    gain = jnp.sum(jnp.exp2(logit - top[None]), axis=0)
-                    total = gain if m is None else total * jnp.exp2(m - top) + gain
-                    m = top
-            top = jnp.max(m, axis=0, keepdims=True)
-            total = jnp.sum(total * jnp.exp2(m - top), axis=0, keepdims=True)
-            score = jnp.sum(jnp.where(jnp.bitwise_and(t, 7) == sub, hit, 0.0), axis=0, keepdims=True)
-            for n, v in enumerate((top, total, score)):
-                for k in range(2):
-                    sbuf[slot, pl.ds(n * 2 + k, 1), :] = v[:, k * W:(k + 1) * W]
-            return carry
-
-        if len(items) == 1:
-            one(0, 0)
-        else:
-            lax.fori_loop(0, len(items), one, 0)
+            for u in range(CH // SUB):
+                logit = logits[pl.ds(first + u * SUB, SUB), :].reshape(G8, 8, T)
+                top = jnp.maximum(m, jnp.max(logit, axis=0))
+                chosen = [logit[r] for r in range(G8)]
+                for b in range(levels):
+                    chosen = [jnp.where(bits[b], chosen[2 * r + 1], chosen[2 * r]) for r in range(len(chosen) // 2)]
+                hit = jnp.where(which == k * (CH // SUB) + u, chosen[0], hit)
+                total = total * jnp.exp2(m - top) + jnp.sum(jnp.exp2(logit - top[None]), axis=0)
+                m = top
+            return m, total, hit
+
+        zero = jnp.zeros((8, T), f32)
+        m, total, hit = lax.fori_loop(0, 2 * B // CH, chunk, (jnp.full((8, T), -jnp.inf, f32), zero, zero))
+        if at is None:
+            return
+        top = jnp.max(m, axis=0, keepdims=True)
+        total = jnp.sum(total * jnp.exp2(m - top), axis=0, keepdims=True)
+        score = jnp.sum(jnp.where(jnp.bitwise_and(t, 7) == sub, hit, 0.0), axis=0, keepdims=True)
+        for n, v in enumerate((top, total, score)):
+            for k in range(2):
+                sbuf[slot, pl.ds(n * 2 + k, 1), :] = v[:, k * W:(k + 1) * W]
+
+    def give_back(items):
         for dx, dz in items:
             for k in ((dz,) if dz != 2 else (2, -2)):
                 if (dx, k) == (0, 0):
@@ -519,21 +535,38 @@
                     send_sem=ssend.at[0], recv_sem=srecv.at[0], device_id=chip(dx, k), device_id_type=MESH)
                 cp.start()
 
-    blocks([(0, 0)])
+    def blocks(items, last):
+        todo = [last] + items[:-1]
+
+        def pair(i, carry):
+            block(place(items, 2 * i), logits1, qt1, place(todo, 2 * i), logits0)
+            block(place(items, 2 * i + 1), logits0, qt0, place(todo, 2 * i + 1), logits1)
+            return carry
+
+        if len(items) == 2:
+            pair(0, 0)
+        else:
+            lax.fori_loop(0, len(items) // 2, pair, 0)
+        give_back(todo)
+
+    block((0, 0), logits0, qt0, None, None)
     qrelay(1)
     qrelay(2)
-    blocks([(-1, 0), (1, 0), (0, -1), (0, 1)])
+    blocks([(-1, 0), (1, 0), (0, -1), (0, 1)], (0, 0))
     qrelay(3)
     qrelay(4)
     qrelay(5)
-    blocks([(-1, -1), (-1, 1), (1, -1), (1, 1)])
+    blocks([(-1, -1), (-1, 1), (1, -1), (1, 1)], (0, 1))
     qrelay(6)
-    blocks([(2, 0), (0, 2)])
     qrelay(7)
+    blocks([(2, 0), (0, 2)], (1, 1))
     qrelay(8)
-    blocks([(2, -1), (2, 1), (-1, 2), (1, 2)])
+    blocks([(2, -1), (2, 1), (-1, 2), (1, 2)], (0, 2))
     qrelay(9)
-    blocks([(2, 2)])
+    block((3, 3), logits1, qt1, (2, 3), logits0)
+    give_back([(1, 2)])
+    block(None, None, None, (3, 3), logits1)
+    give_back([(2, 2)])
 
     arrived(rows_in.at[pl.ds(0, len(near))], nrecv.at[0])
     arrived(counts_in.at[pl.ds(0, len(near))], crecv.at[0])
@@ -623,6 +656,9 @@
             pltpu.VMEM((2 * B, T // 2), jnp.float32),
             pltpu.VMEM((16, T, E), jnp.bfloat16),
             pltpu.VMEM((E, T), jnp.bfloat16),
+            pltpu.VMEM((E, T), jnp.bfloat16),
+            pltpu.VMEM((2 * B, T), jnp.float32),
+            pltpu.VMEM((2 * B, T), jnp.float32),
             pltpu.VMEM((20, 1, T), jnp.int32),
             pltpu.VMEM((16, 8, T // 2), jnp.float32),
             pltpu.VMEM((20, 8, T // 2), jnp.float32),
@@ -647,10 +683,27 @@
 def body(
     tokens, w_hidden, w_out, bank, item_ids, log_freq, positives, new_items, new_owner, queue_head
 ):
-    return tower(
+    results = tower(
         tokens, w_hidden, w_out, bank, log_freq.reshape(-1, 128), item_ids.reshape(-1, 128),
         positives, new_items, new_owner.reshape(1, -1), queue_head,
     )
+    return settle(results)
+
+
+def settle_kernel(loss_in, bank_in, loss_out, bank_out):
+    loss_out[...] = loss_in[...]
+    bank_out[...] = bank_in[...]
+
+
+def settle(results):
+    vmem = pl.BlockSpec(memory_space=pltpu.VMEM)
+    return pl.pallas_call(
+        settle_kernel,
+        out_shape=tuple(jax.ShapeDtypeStruct(r.shape, r.dtype) for r in results),
+        in_specs=[vmem, vmem],
+        out_specs=(vmem, vmem),
+        name="settle",
+    )(*results)
 
 
 def solution(mesh):

time: 78.9 us -> 77.3 us (0.980)
  local copies, waits for them, and re-layouts: 3.07 us -> 0 us
  Pallas kernels: 74.3 us -> 75.9 us
    unnamed x2 -> x0, local copies, waits for them, and re-layouts: 3.07 us -> none
    pallas_call x0 -> x1, Pallas kernels: none -> 1.88 us  [settle(): pl.pallas_call(settle_kernel, out_shape=tuple((jax.ShapeDtypeStruct(r.sha...]
where the time goes in v5:
time: 77.3 us; the launch traced here: 77.2 us
  Pallas kernels  75.9 us (98%)
  between operations  1.29 us (2%)
    pallas_call x1, Pallas kernels, tower(): pl.pallas_call(tower_kernel, out_shape=(jax.ShapeDtypeStruct((1, T), jnp....  74 us
    pallas_call x1, Pallas kernels, settle(): pl.pallas_call(settle_kernel, out_shape=tuple((jax.ShapeDtypeStruct(r.sha...  1.88 us

profile of v5, /device:TPU:2, one launch (start us, length us, event | category | flops | bytes accessed | tf_op | source)
XLA Modules:
  0.0 77.2 jit_solution(14918166114488594278)
XLA Ops:
  1.3 74.0 %tower.1 = (f32[1,256]{1,0:T(1,128)}, bf16[1024,256]{1,0:T(8,128)(2,1)}) custom-call(bf16[1,1024,4096]{2,1,0:T(8,128)(2,1)} %tok_hbm.1, bf16[128,1024]{1,0:T(8,128)(2,1)} %w_hbm.1, bf16[1024,256]{1,0:T(8,128)(2,1)} %wo_ref.1, bf16[1024,256]{1,0:T(8,128)(2,1)} %bank_hbm.1, bf16[8192,128]{1,0:T(8,128)(2,1)} %bitcast.3, s32[8,128]{1,0:T(8,128)} %bitcast.4, ...), custom_call_target="tpu_custom_call" | custom-call | tf_op jit(solution)/shard_map/tower/pallas_call | solution.py:642
  75.3 1.9 %settle.1 = (f32[1,256]{1,0:T(1,128)}, bf16[1024,256]{1,0:T(8,128)(2,1)}) custom-call(f32[1,256]{1,0:T(1,128)} %get-tuple-element.4.loss_in, bf16[1024,256]{1,0:T(8,128)(2,1)} %get-tuple-element.5.bank_in), custom_call_target="tpu_custom_call" | custom-call | tf_op jit(solution)/shard_map/settle/pallas_call | solution.py:700

commit v6 on v5

--- a/solution.py
+++ b/solution.py
@@ -148,9 +148,6 @@
     for h in (0, 1):
         for step in (1, -1):
             send(h, 0, 0, None, True, step, (-step, 0))
-    for h in (0, 1):
-        for step in (1, -1):
-            send(h, 0, 0, None, False, step, (0, -step))
 
     swaps = []
 
@@ -240,20 +237,27 @@
             arrived(offb.at[pl.ds(0, (ny - 1) * OR), :], orecv.at[0])
         swap(offb)
 
-    def relay(g):
+    def take(g):
         for f, s in groups[g]:
             for h in (0, 1):
                 for p in pieces(f, s):
                     wait_link(h, f, s, p)
-                for p in pieces(f, s):
                     to_partner(h, f, s, p)
-                if s == 0 and f != 2:
-                    send(h, f, 0, 0 if f == -1 else 1, True, -f, (2, 0))
-                if s == 0:
-                    for step in (1, -1):
-                        send(h, f, 0, None, False, step, (f, -step))
-                elif s != 2:
-                    send(h, f, s, 0 if s == -1 else 1, False, -s, (f, 2))
+
+    def onward_first():
+        for f in (-1, 1):
+            for h in (0, 1):
+                send(h, f, 0, 0 if f == -1 else 1, True, -f, (2, 0))
+
+    def across(f):
+        for h in (0, 1):
+            for step in (1, -1):
+                send(h, f, 0, None, False, step, (f, -step))
+
+    def onward_second(f):
+        for s in (-1, 1):
+            for h in (0, 1):
+                send(h, f, s, 0 if s == -1 else 1, False, -s, (f, 2))
 
     def mm(g):
         items = groups[g]
@@ -282,30 +286,37 @@
         lax.fori_loop(0, 2 * len(items), step, 0)
 
     pack()
+    across(0)
     mm(0)
     off_start()
-    relay(1)
-    off_step(0)
-    off_step(1)
-    relay(2)
+    take(1)
+    onward_first()
+    across(-1)
+    for j in range(4):
+        off_step(j)
+    off_end()
+    take(2)
+    across(1)
     mm(1)
-    off_step(2)
-    off_step(3)
-    off_end()
-    relay(3)
+    take(3)
     mm(2)
-    relay(4)
+    take(4)
+    onward_second(0)
+    across(2)
     mm(3)
-    relay(5)
+    take(5)
+    onward_second(-1)
     mm(4)
-    relay(6)
+    off_collect()
+    take(6)
+    onward_second(1)
     mm(5)
-    relay(7)
+    take(7)
+    onward_second(2)
     mm(6)
-    off_collect()
-    relay(8)
+    take(8)
     mm(7)
-    relay(9)
+    take(9)
     mm(8)
     mm(9)
 

time: 77.3 us -> 75.3 us (0.974)
  Pallas kernels: 75.9 us -> 73.8 us
    pallas_call x1, Pallas kernels: 74 us -> 72 us  [tower(): pl.pallas_call(tower_kernel, out_shape=(jax.ShapeDtypeStruct((1, T), jnp....]
where the time goes in v6:
time: 75.3 us; the launch traced here: 75.1 us
  Pallas kernels  73.8 us (98%)
  between operations  1.29 us (2%)
    pallas_call x1, Pallas kernels, tower(): pl.pallas_call(tower_kernel, out_shape=(jax.ShapeDtypeStruct((1, T), jnp....  72 us
    pallas_call x1, Pallas kernels, settle(): pl.pallas_call(settle_kernel, out_shape=tuple((jax.ShapeDtypeStruct(r.sha...  1.88 us

profile of v6, /device:TPU:2, one launch (start us, length us, event | category | flops | bytes accessed | tf_op | source)
XLA Modules:
  0.0 75.1 jit_solution(4029254759855531664)
XLA Ops:
  1.3 72.0 %tower.1 = (f32[1,256]{1,0:T(1,128)}, bf16[1024,256]{1,0:T(8,128)(2,1)}) custom-call(bf16[1,1024,4096]{2,1,0:T(8,128)(2,1)} %tok_hbm.1, bf16[128,1024]{1,0:T(8,128)(2,1)} %w_hbm.1, bf16[1024,256]{1,0:T(8,128)(2,1)} %wo_ref.1, bf16[1024,256]{1,0:T(8,128)(2,1)} %bank_hbm.1, bf16[8192,128]{1,0:T(8,128)(2,1)} %bitcast.3, s32[8,128]{1,0:T(8,128)} %bitcast.4, ...), custom_call_target="tpu_custom_call" | custom-call | tf_op jit(solution)/shard_map/tower/pallas_call | solution.py:653
  73.2 1.9 %settle.1 = (f32[1,256]{1,0:T(1,128)}, bf16[1024,256]{1,0:T(8,128)(2,1)}) custom-call(f32[1,256]{1,0:T(1,128)} %get-tuple-element.4.loss_in, bf16[1024,256]{1,0:T(8,128)(2,1)} %get-tuple-element.5.bank_in), custom_call_target="tpu_custom_call" | custom-call | tf_op jit(solution)/shard_map/settle/pallas_call | solution.py:711

commit v7 on v6

--- a/solution.py
+++ b/solution.py
@@ -122,7 +122,7 @@
         pl.semaphore_signal(barrier, inc=1, device_id=p, device_id_type=MESH)
 
     groups = [[(0, 0)], [(-1, 0), (1, 0)], [(0, -1), (0, 1)], [(2, 0)],
-              [(-1, -1), (-1, 1)], [(1, -1), (1, 1)], [(0, 2)], [(2, -1), (2, 1)], [(-1, 2), (1, 2)], [(2, 2)]]
+              [(-1, -1), (-1, 1)], [(1, -1), (1, 1)], [(0, 2)], [(2, -1), (2, 1)], [(-1, 2)], [(1, 2)], [(2, 2)]]
 
     tok_wait = {}
     n = 0
@@ -259,15 +259,18 @@
             for h in (0, 1):
                 send(h, f, s, 0 if s == -1 else 1, False, -s, (f, 2))
 
-    def mm(g):
-        items = groups[g]
-        for f, s in items:
+    def ready(g):
+        for f, s in groups[g]:
             for h in (0, 1):
                 dx, dz = (f, s) if h == 0 else (s, f)
                 if (dx, dz) in tok_wait:
                     tok_wait.pop((dx, dz)).wait()
                 for p in pieces(f, s):
                     wait_partner(h, f, s, p)
+
+    def mm(g):
+        items = groups[g]
+        ready(g)
 
         def step(i, carry):
             h = lax.rem(i, 2)
@@ -318,7 +321,9 @@
     mm(7)
     take(9)
     mm(8)
+    take(10)
     mm(9)
+    ready(10)
 
     far = [(i, k) for i in offs for k in (0, -1, 1, 2, -2) if (i, k) != (0, 0)]
 
@@ -362,11 +367,15 @@
     def quarter(step):
         return pl.ds(pl.multiple_of(lax.rem(y + step + 4, 4) * T, T), T)
 
+    far_block = block_of(0, 2, 2)
+    far_rows = pl.ds(pl.multiple_of(far_block * (2 * R), 2 * R), 2 * R)
+
     def partial(step):
         rs = quarter(step)
         total = None
         for h in (0, 1):
-            hid = jnp.maximum(acc[h, rs, :], 0.0).astype(jnp.bfloat16)
+            end = jnp.dot(tok[far_block, rs, :], wbuf[h, far_rows, :], preferred_element_type=jnp.float32)
+            hid = jnp.maximum(acc[h, rs, :] + end, 0.0).astype(jnp.bfloat16)
             d = jnp.dot(hid, wo_ref[pl.ds(h * C, C), :], preferred_element_type=jnp.float32)
             total = d if total is None else total + d
         part[rs, :] = total
@@ -572,8 +581,9 @@
     qrelay(7)
     blocks([(2, 0), (0, 2)], (1, 1))
     qrelay(8)
+    qrelay(9)
     blocks([(2, -1), (2, 1), (-1, 2), (1, 2)], (0, 2))
-    qrelay(9)
+    qrelay(10)
     block((3, 3), logits1, qt1, (2, 3), logits0)
     give_back([(1, 2)])
     block(None, None, None, (3, 3), logits1)

time: 75.3 us -> 74.4 us (0.988)
  Pallas kernels: 73.8 us -> 73 us
    pallas_call x1, Pallas kernels: 72 us -> 71.1 us  [tower(): pl.pallas_call(tower_kernel, out_shape=(jax.ShapeDtypeStruct((1, T), jnp....]
where the time goes in v7:
time: 74.4 us; the launch traced here: 74.2 us
  Pallas kernels  73 us (98%)
  between operations  1.29 us (2%)
    pallas_call x1, Pallas kernels, tower(): pl.pallas_call(tower_kernel, out_shape=(jax.ShapeDtypeStruct((1, T), jnp....  71.1 us
    pallas_call x1, Pallas kernels, settle(): pl.pallas_call(settle_kernel, out_shape=tuple((jax.ShapeDtypeStruct(r.sha...  1.88 us

profile of v7, /device:TPU:2, one launch (start us, length us, event | category | flops | bytes accessed | tf_op | source)
XLA Modules:
  0.0 74.2 jit_solution(1055731308590721072)
XLA Ops:
  1.3 71.1 %tower.1 = (f32[1,256]{1,0:T(1,128)}, bf16[1024,256]{1,0:T(8,128)(2,1)}) custom-call(bf16[1,1024,4096]{2,1,0:T(8,128)(2,1)} %tok_hbm.1, bf16[128,1024]{1,0:T(8,128)(2,1)} %w_hbm.1, bf16[1024,256]{1,0:T(8,128)(2,1)} %wo_ref.1, bf16[1024,256]{1,0:T(8,128)(2,1)} %bank_hbm.1, bf16[8192,128]{1,0:T(8,128)(2,1)} %bitcast.3, s32[8,128]{1,0:T(8,128)} %bitcast.4, ...), custom_call_target="tpu_custom_call" | custom-call | tf_op jit(solution)/shard_map/tower/pallas_call | solution.py:663
  72.4 1.9 %settle.1 = (f32[1,256]{1,0:T(1,128)}, bf16[1024,256]{1,0:T(8,128)(2,1)}) custom-call(f32[1,256]{1,0:T(1,128)} %get-tuple-element.4.loss_in, bf16[1024,256]{1,0:T(8,128)(2,1)} %get-tuple-element.5.bank_in), custom_call_target="tpu_custom_call" | custom-call | tf_op jit(solution)/shard_map/settle/pallas_call | solution.py:721
